TPU v7x, 128 devices: a whole 4x4x4 slice. The times are simulated.
128 devices in a mesh: len: 32 (over x, y, core), mem: 4 (over z).
Axes of the slice: x: 4, y: 4, z: 4, core: 2. Of those that a mesh axis runs over, the one named last changes fastest.
Arguments:
- phase_left: float32 [32, 1048576], P('mem', 'len'), may hold values from -3.140625 to 3.140625
- phase_right: float32 [32, 1048576], P('mem', 'len'), may hold values from -3.140625 to 3.140625
- roughness: float32 [32], P('mem'), may hold values from 0.1 to 10
- waviness: float32 [32], P('mem'), may hold values from 1.5 to 2.5
- coherence: float32 [32], P('mem'), may hold values from 32 to 512
Outputs:
- profile: float32 [2, 32, 1048576], P(None, 'mem', 'len')
- r_factor: float32 [32, 32], replicated
All inputs are finite; a program needn't handle non-finite values.
Results may differ from a plain program's by a relative error of at most 0.0003.
Values sent between devices are 32-bit elements; how exact they have to be, the bound alone decides.
A program may use at most 128 MiB of HBM per device.

v0:
```python
import math

import jax
import jax.numpy as jnp
from jax import lax
from jax.sharding import PartitionSpec as P

OUTER = 1024
INNER = 1024
ANCHOR = 64


highest = lax.Precision.HIGHEST


def merged(shard, axis, combine):
    everything = lax.all_gather(shard, axis)
    leading = everything[0]

    def step(k, so_far):
        return combine(so_far, everything[k])

    return lax.fori_loop(1, lax.axis_size(axis), step, leading)


def dft_tables(length):
    index = lax.iota(jnp.int32, length)
    product = index[:, None] * index[None, :] % length
    phase_angle = product.astype(jnp.float32) * (2.0 * math.pi / length)
    return (jnp.cos(phase_angle), jnp.sin(phase_angle))


def spectra_of(phase_left, phase_right, roughness, waviness, coherence, freq):
    amplitude = jnp.sqrt(2.0 * roughness * (waviness - 1.0) / ANCHOR)[:, None] * (
        (freq + ANCHOR) / ANCHOR
    ) ** (-0.5 * waviness[:, None])
    freq_ratio = freq / coherence[:, None]
    coherent = 1.0 / (1.0 + freq_ratio * freq_ratio)
    incoherent = freq_ratio * jnp.sqrt(2.0 + freq_ratio * freq_ratio) * coherent
    cos_left = jnp.cos(phase_left)
    sin_left = jnp.sin(phase_left)
    cos_right = jnp.cos(phase_right)
    sin_right = jnp.sin(phase_right)
    real_part = jnp.stack(
        [amplitude * cos_left, amplitude * (coherent * cos_left + incoherent * cos_right)]
    )
    imag_part = jnp.stack(
        [amplitude * sin_left, amplitude * (coherent * sin_left + incoherent * sin_right)]
    )
    return (real_part, imag_part)


def upper_of(gram_matrix):
    return jnp.linalg.cholesky(gram_matrix).T


def combine_factors(upper_a, upper_b):
    gram_matrix = jnp.dot(upper_a.T, upper_a, precision=highest) + jnp.dot(
        upper_b.T, upper_b, precision=highest
    )
    return upper_of(gram_matrix)


def gram_of(snapshot):
    return jnp.einsum("tmr,tnr->mn", snapshot, snapshot, precision=highest)


def per_device(phase_left, phase_right, roughness, waviness, coherence):
    shards = lax.axis_size("len")
    my_index = lax.axis_index("len")
    local_members, local_len = phase_left.shape
    columns = 2 * local_members
    outer_block = OUTER // shards
    inner_block = INNER // shards

    def to_rows(part):
        shaped = part.reshape(2, local_members, inner_block, OUTER)
        return jnp.transpose(shaped, (2, 3, 0, 1)).reshape(
            inner_block, shards, outer_block * columns
        )

    inner_cos, inner_sin = dft_tables(INNER)
    freq = (my_index * local_len + lax.iota(jnp.int32, local_len)).astype(jnp.float32)[None, :]
    real_part, imag_part = spectra_of(phase_left, phase_right, roughness, waviness, coherence, freq)
    pieces = (
        lax.all_to_all(to_rows(real_part), "len", split_axis=1, concat_axis=0, tiled=True),
        lax.all_to_all(to_rows(imag_part), "len", split_axis=1, concat_axis=0, tiled=True),
    )
    real_in = pieces[0].reshape(INNER, -1)
    imag_in = pieces[1].reshape(INNER, -1)
    real_out = jnp.dot(inner_cos, real_in, precision=highest) - jnp.dot(
        inner_sin, imag_in, precision=highest
    )
    imag_out = jnp.dot(inner_cos, imag_in, precision=highest) + jnp.dot(
        inner_sin, real_in, precision=highest
    )
    row_index = lax.iota(jnp.int32, INNER)[:, None]
    outer_index = (my_index * outer_block + lax.iota(jnp.int32, outer_block))[None, :]
    twist = (row_index * outer_index % (OUTER * INNER)).astype(jnp.float32) * (
        2.0 * math.pi / (OUTER * INNER)
    )
    twist_cos = jnp.repeat(jnp.cos(twist), columns, axis=1)
    twist_sin = jnp.repeat(jnp.sin(twist), columns, axis=1)
    rot_real = (real_out * twist_cos - imag_out * twist_sin).reshape(
        shards, inner_block, outer_block * columns
    )
    rot_imag = (real_out * twist_sin + imag_out * twist_cos).reshape(
        shards, inner_block, outer_block * columns
    )
    outer_cos, outer_sin = dft_tables(OUTER)
    outer_cos = outer_cos.reshape(OUTER, shards, outer_block)
    outer_sin = outer_sin.reshape(OUTER, shards, outer_block)
    pieces = (
        lax.all_to_all(rot_real, "len", split_axis=0, concat_axis=0, tiled=True),
        lax.all_to_all(rot_imag, "len", split_axis=0, concat_axis=0, tiled=True),
    )
    item_count = pieces[0].shape[1]
    real_in = pieces[0].reshape(shards, item_count, outer_block, columns)
    imag_in = pieces[1].reshape(shards, item_count, outer_block, columns)
    first = jnp.einsum("jqa,qiac->cij", outer_cos, real_in, precision=highest)
    second = jnp.einsum("jqa,qiac->cij", outer_sin, imag_in, precision=highest)
    profile_block = first - second
    outgoing = jnp.transpose(
        profile_block.reshape(columns, inner_block, shards, outer_block), (2, 0, 1, 3)
    ).reshape(shards, -1)
    arrived = lax.all_to_all(outgoing, "len", split_axis=0, concat_axis=0, tiled=True)
    profile = jnp.transpose(
        arrived.reshape(shards, columns, inner_block, outer_block), (1, 3, 0, 2)
    ).reshape(2, local_members, local_len)
    scale = 1.0 / math.sqrt(2.0 * OUTER * INNER)
    snapshot = profile_block.reshape(2, local_members, inner_block * OUTER) * scale
    gathered = lax.all_gather(snapshot, "mem", axis=1, tiled=True)
    gram_local = gram_of(gathered)
    r_factor = merged(upper_of(gram_local), "len", combine_factors)
    return (profile, r_factor)


def solution(mesh):
    placed = (P("mem", "len"), P("mem", "len"), P("mem"), P("mem"), P("mem"))
    return jax.shard_map(
        per_device,
        mesh=mesh,
        in_specs=placed,
        out_specs=(P(None, "mem", "len"), P()),
        check_vma=False,
    )
```

profile of v0, /device:TPU:1, one launch (start us, length us, event | category | flops | bytes accessed | tf_op | source)
XLA Modules:
  0.0 587.4 jit_solution(10897964945653055579)
XLA Ops:
  7.2 4.7 fusion.78
  12.6 8.0 %add_multiply_fusion.1 = (f32[8,32768]{1,0:T(8,128)S(1)}, f32[8,32768]{1,0:T(8,128)S(1)}, f32[8,32768]{1,0:T(8,128)}, f32[8,32768]{1,0:T(8,128)S(1)}) fusion(f32[8,32768]{1,0:T(8,128)} %param.9, f32[8,32768]{1,0:T(8,128)S(1)} %get-tuple-element.124, f32[8]{0:T(128)} %param.12, f32[32768]{0:T(1024)S(1)} %add_convert_fusion, f32[8]{0:T(128)S(1)} %get-tuple-element.129, ...), kind=kLoop, calls=%fused_computation.57 | loop fusion | flops 4718592 | bytes 7602272 | tf_op jit(solution)/shard_map/mul | solution.py:45
  22.0 6.2 %copy.59 = f32[32,1024,2,8]{0,3,2,1:T(8,128)} copy(f32[32,1024,2,8]{1,0,3,2:T(8,128)S(1)} %maximum_bitcast_fusion) | data formatting | bytes 4194304 | tf_op jit(solution)/shard_map/transpose | solution.py:78
  28.3 6.2 %copy.60 = f32[32,32,512]{2,0,1:T(8,128)} copy(f32[32,32,512]{0,2,1:T(8,128)} %bitcast.112) | data formatting | bytes 4194304 | tf_op jit(solution)/shard_map/reshape | solution.py:78
  34.5 8.8 %all-to-all-start = ((f32[32,32,512]{2,0,1:T(8,128)}), f32[32,32,512]{2,0,1:T(8,128)}, u32[]{:S(2)}, u32[]{:S(2)}) async-start(f32[32,32,512]{2,0,1:T(8,128)} %copy.60), calls=%async_computation | async-start | bytes 4194304 | tf_op jit(solution)/shard_map/all_to_all | solution.py:86
  44.8 6.2 %copy.61 = f32[32,1024,2,8]{0,3,2,1:T(8,128)} copy(f32[32,1024,2,8]{1,0,3,2:T(8,128)S(1)} %maximum_bitcast_fusion.1) | data formatting | bytes 4194304 | tf_op jit(solution)/shard_map/transpose | solution.py:78
  51.0 6.3 %copy.62 = f32[32,32,512]{2,0,1:T(8,128)} copy(f32[32,32,512]{0,2,1:T(8,128)} %bitcast.113) | data formatting | bytes 4194304 | tf_op jit(solution)/shard_map/reshape | solution.py:78
  57.3 14.4 %all-to-all-done = f32[32,32,512]{2,0,1:T(8,128)} async-done(((f32[32,32,512]{2,0,1:T(8,128)}), f32[32,32,512]{2,0,1:T(8,128)}, u32[]{:S(2)}, u32[]{:S(2)}) %all-to-all-start) | async-done | bytes 2097184 | tf_op jit(solution)/shard_map/all_to_all | solution.py:86
  71.6 5.2 all-to-all-start.1
  81.8 23.7 %fusion.29 = f32[1024,512]{1,0:T(8,128)S(1)} fusion(f32[1024,512]{1,0:T(8,128)} %bitcast.7), kind=kOutput, calls=%fused_computation.45 | convolution fusion | flops 6457131008 | bytes 4194304 | tf_op jit(solution)/shard_map/dot_general | solution.py:91
  105.5 24.1 %fusion.27 = f32[1024,512]{1,0:T(8,128)S(1)} fusion(f32[1024,512]{1,0:T(8,128)} %bitcast.12), kind=kOutput, calls=%fused_computation.44 | convolution fusion | flops 6457131008 | bytes 4194304 | tf_op jit(solution)/shard_map/dot_general | solution.py:94
  129.6 24.2 %fusion.35 = f32[1024,512]{1,0:T(8,128)S(1)} fusion(f32[1024,512]{1,0:T(8,128)S(1)} %fusion.29, f32[1024,512]{1,0:T(8,128)} %bitcast.12), kind=kOutput, calls=%fused_computation.48 | convolution fusion | flops 6457655296 | bytes 6291456 | tf_op jit(solution)/shard_map/dot_general | solution.py:91
  153.8 25.8 %multiply_subtract_fusion = (f32[1024,512]{1,0:T(8,128)}, f32[1024,512]{1,0:T(8,128)S(1)}) fusion(f32[1024,512]{1,0:T(8,128)S(1)} %copy-done.2, f32[1024,512]{1,0:T(8,128)S(1)} %fusion.35, f32[1024,512]{1,0:T(8,128)S(1)} %copy-done.1, f32[1024,512]{1,0:T(8,128)S(1)} %fusion.27, f32[1024,512]{1,0:T(8,128)} %bitcast.7), kind=kOutput, calls=%fused_computation.41 | convolution fusion | flops 6460801024 | bytes 14680064 | tf_op jit(solution)/shard_map/dot_general | solution.py:94
  179.6 35.5 %all_to_all.50 = f32[32,32,512]{2,1,0:T(8,128)} all-to-all(f32[32,32,512]{2,1,0:T(8,128)S(1)} %bitcast.125), channel_id=1, replica_groups=mesh['len'=32,'mem'=4] {'len'}, dimensions={0} | all-to-all | bytes 4194304 | tf_op jit(solution)/shard_map/all_to_all | solution.py:115
  215.1 4.0 all-to-all-start.2
  219.1 6.3 %copy.68 = f32[32,32,512]{0,2,1:T(8,128)} copy(f32[32,32,512]{2,1,0:T(8,128)} %all_to_all.50) | data formatting | bytes 4194304 | tf_op jit(solution)/shard_map/all_to_all | solution.py:115
  225.4 35.0 %fusion.10 = f32[32,16,1024,1]{2,1,3,0:T(8,128)} fusion(f32[32,32,32,16]{0,3,2,1:T(8,128)} %bitcast.117, s32[32,32]{0,1:T(8,128)S(1)} %multiply_add_fusion.1), kind=kOutput, calls=%fused_computation.24 | convolution fusion | flops 6457131008 | bytes 4198400 | tf_op jit(solution)/shard_map/jqa,qiac->cij/dot_general | solution.py:121
  260.4 4.7 copy.65
  265.1 35.5 %broadcast_multiply_fusion = (f32[16,32,1024]{2,0,1:T(8,128)S(1)}, f32[16,32,1024]{2,0,1:T(8,128)}) fusion(f32[32,16,1024,1]{2,1,3,0:T(8,128)} %fusion.10, f32[32,32,32,16]{0,3,2,1:T(8,128)} %bitcast.116, s32[32,32]{0,1:T(8,128)S(1)} %multiply_add_fusion.1), kind=kOutput, calls=%fused_computation.55 | convolution fusion | flops 6458179584 | bytes 8392704 | tf_op jit(solution)/shard_map/jqa,qiac->cij/dot_general | solution.py:120
  303.4 6.5 %reshape.117 = f32[16,32,32,32]{3,2,0,1:T(8,128)} reshape(f32[16,32,1024]{2,0,1:T(8,128)} %get-tuple-element.131) | data formatting | bytes 4194304 | tf_op jit(solution)/shard_map/reshape | solution.py:124
  309.9 11.7 %copy.90 = f32[16,32,32,32]{3,1,0,2:T(8,128)} copy(f32[16,32,32,32]{3,2,0,1:T(8,128)} %reshape.117) | data formatting | bytes 4194304 | tf_op jit(solution)/shard_map/reshape | solution.py:124
  321.6 7.7 %all_to_all.44 = f32[32,1,16384]{2,1,0:T(1,128)} reshape(f32[32,16,32,32]{3,2,1,0:T(8,128)} %bitcast.114) | data formatting | bytes 4194304 | tf_op jit(solution)/shard_map/all_to_all | solution.py:126
  329.4 8.0 %all-to-all-start.4 = ((f32[32,1,16384]{2,1,0:T(1,128)}), f32[32,1,16384]{2,1,0:T(1,128)}, u32[]{:S(2)}, u32[]{:S(2)}) async-start(f32[32,1,16384]{2,1,0:T(1,128)} %all_to_all.44), calls=%async_computation.4 | async-start | bytes 4194304 | tf_op jit(solution)/shard_map/all_to_all | solution.py:126
  337.4 28.1 %all-to-all-done.4 = f32[32,1,16384]{2,1,0:T(1,128)} async-done(((f32[32,1,16384]{2,1,0:T(1,128)}), f32[32,1,16384]{2,1,0:T(1,128)}, u32[]{:S(2)}, u32[]{:S(2)}) %all-to-all-start.4) | async-done | bytes 2097184 | tf_op jit(solution)/shard_map/all_to_all | solution.py:126
  365.6 6.7 %reduce.4 = f32[32,16384]{1,0:T(8,128)S(1)} reduce(f32[32,1,16384]{2,1,0:T(1,128)} %all-to-all-done.4, f32[]{:T(128)} %constant.131), dimensions={1}, to_apply=%all_to_all.43.reduce_sub_computation | reduce | bytes 4194308 | tf_op jit(solution)/shard_map/all_to_all | solution.py:126
  372.3 4.8 reshape.118
  377.1 10.6 %copy.71 = f32[16,32,32,32]{3,2,1,0:T(8,128)} copy(f32[16,32,32,32]{1,3,0,2:T(8,128)} %bitcast.115) | data formatting | bytes 4194304 | tf_op jit(solution)/shard_map/transpose | solution.py:127
  387.7 7.0 %reshape.119 = f32[2,8,32768]{2,1,0:T(8,128)} reshape(f32[16,32,32,32]{3,2,1,0:T(8,128)} %copy.71) | data formatting | bytes 4194304 | tf_op jit(solution)/shard_map/reshape | solution.py:129
  394.7 10.6 %convolution_bitcast_fusion = f32[32,32]{1,0:T(8,128)S(1)} fusion(f32[2,32,32768]{2,1,0:T(8,128)} %all-gather.3.cloned.1.call-done), kind=kOutput, calls=%fused_computation.50 | convolution fusion | flops 805306368 | bytes 8392704 | tf_op jit(solution)/shard_map/tmr,tnr->mn/dot_general | solution.py:65
  405.4 2.9 cholesky.55
  409.8 23.1 %all-gather = f32[1024,32]{1,0:T(8,128)S(1)} all-gather(f32[32,32]{1,0:T(8,128)S(1)} %copy.74), channel_id=2, replica_groups=mesh['len'=32,'mem'=4] {'len'}, dimensions={0}, use_global_device_ids=true | all-gather | bytes 135168 | tf_op jit(solution)/shard_map/all_gather | solution.py:17
  433.0 146.6 %while.15 = (s32[]{:T(128)}, f32[32,32]{0,1:T(8,128)S(1)}, f32[32,32,32]{2,1,0:T(8,128)S(1)}, s32[]{:T(128)}, s32[]{:T(128)}, /*index=5*/s32[]{:T(128)}) while((s32[]{:T(128)}, f32[32,32]{0,1:T(8,128)S(1)}, f32[32,32,32]{2,1,0:T(8,128)S(1)}, s32[]{:T(128)}, s32[]{:T(128)}, /*index=5*/s32[]{:T(128)}) %tuple.65), condition=%wide.region_3.5_spmd, body=%wide.region_2.4_spmd.sunk | while | flops 795684 | bytes 78197 | solution.py:23
  (284 shorter events, 158.9 us)
Async XLA Ops:
  34.5 8.8 %copy-start = (f32[8,32768]{1,0:T(8,128)S(1)}, f32[8,32768]{1,0:T(8,128)}, u32[]{:S(2)}) copy-start(f32[8,32768]{1,0:T(8,128)} %get-tuple-element.122) | copy-start | bytes 3145732
  34.5 37.1 %all-to-all-start = ((f32[32,32,512]{2,0,1:T(8,128)}), f32[32,32,512]{2,0,1:T(8,128)}, u32[]{:S(2)}, u32[]{:S(2)}) async-start(f32[32,32,512]{2,0,1:T(8,128)} %copy.60), calls=%async_computation | async-start | bytes 4194304 | tf_op jit(solution)/shard_map/all_to_all | solution.py:86
  71.6 33.8 %all-to-all-start.1 = ((f32[32,32,512]{2,0,1:T(8,128)}), f32[32,32,512]{2,0,1:T(8,128)}, u32[]{:S(2)}, u32[]{:S(2)}) async-start(f32[32,32,512]{2,0,1:T(8,128)} %copy.62), calls=%async_computation.1 | async-start | bytes 4194304 | tf_op jit(solution)/shard_map/all_to_all | solution.py:87
  129.6 24.2 %copy-start.1 = (f32[1024,512]{1,0:T(8,128)S(1)}, f32[1024,512]{1,0:T(8,128)}, u32[]{:S(2)}) copy-start(f32[1024,512]{1,0:T(8,128)} %copy.63) | copy-start | bytes 6291460
  129.6 24.2 %copy-start.2 = (f32[1024,512]{1,0:T(8,128)S(1)}, f32[1024,512]{1,0:T(8,128)}, u32[]{:S(2)}) copy-start(f32[1024,512]{1,0:T(8,128)} %copy.64) | copy-start | bytes 6291460
  215.1 45.3 %all-to-all-start.2 = ((f32[32,32,512]{2,1,0:T(8,128)}), f32[32,32,512]{2,1,0:T(8,128)S(1)}, u32[]{:S(2)}, u32[]{:S(2)}) async-start(f32[32,32,512]{2,1,0:T(8,128)} %bitcast.124), calls=%async_computation.2 | async-start | bytes 4194304 | tf_op jit(solution)/shard_map/all_to_all | solution.py:114
  219.1 175.6 %all-gather.3.cloned.1.call-start = ((), (), s32[]{:S(2)}) async-start(), calls=%async_computation.5 | async-start | bytes 10485760 | tf_op jit(solution)/shard_map/all_gather | solution.py:132
  329.4 36.2 %all-to-all-start.4 = ((f32[32,1,16384]{2,1,0:T(1,128)}), f32[32,1,16384]{2,1,0:T(1,128)}, u32[]{:S(2)}, u32[]{:S(2)}) async-start(f32[32,1,16384]{2,1,0:T(1,128)} %all_to_all.44), calls=%async_computation.4 | async-start | bytes 4194304 | tf_op jit(solution)/shard_map/all_to_all | solution.py:126
Sparse Core Ops, SparseCore 0:
  303.6 85.3 all-gather.2
where the time goes:
time: 596 us; the launch traced here: 587 us
  matrix products  190 us (32%)
  other arithmetic  153 us (26%)
  local copies, waits for them, and re-layouts  102 us (17%)
  blocking collectives  58.7 us (10%)
  waiting for transfers between devices  42.5 us (7%)
  starting transfers between devices  26 us (4%)
  between operations  14.5 us (2%)
    another operation x96, other arithmetic, upper_of(): return jnp.linalg.cholesky(gram_matrix).T  115 us
    all_to_all x1, blocking collectives, per_device(): lax.all_to_all(rot_imag, 'len', split_axis=0, concat_axis=0, tiled=True)  35.5 us
    dot_general x1, matrix products, per_device(): first = jnp.einsum('jqa,qiac->cij', outer_cos, real_in, precision=highest)  35.5 us
    dot_general x1, matrix products, per_device(): second = jnp.einsum('jqa,qiac->cij', outer_sin, imag_in, precision=highest)  35 us
    all_to_all x1, waiting for transfers between devices, per_device(): lax.all_to_all(outgoing, 'len', split_axis=0, concat_axis=0, tiled=True)  28.1 us
    dot_general x1, matrix products, per_device(): jnp.dot(inner_sin, real_in, precision=highest)  25.8 us
    dot_general x1, matrix products, per_device(): jnp.dot(inner_sin, imag_in, precision=highest)  24.2 us
    dot_general x1, matrix products, per_device(): jnp.dot(inner_cos, imag_in, precision=highest)  24.1 us
  transfers between devices with their start and end apart: 5, of which 2 were waited for; matrix products, arithmetic and copies ran while one was open for 22% of the time, Pallas kernels for 0%

commit v1 on v0

v1 whole, which is shorter than its diff:
```python
import functools
import math

import jax
import jax.numpy as jnp
import ml_dtypes
import numpy as np
from jax import lax
from jax.experimental import pallas as pl
from jax.experimental.pallas import tpu as pltpu
from jax.sharding import PartitionSpec as P

ANCHOR = 64
POINTS = 1048576
LEN = 32
MEM = 4
ROWS = 128
LANES = 128
F32 = jnp.float32
BF16 = jnp.bfloat16
MESH = pl.DeviceIdType.MESH
VMEM_LIMIT = 56 * 1024 * 1024


def halves(table):
    table = np.asarray(table, np.float64)
    high = table.astype(np.float32).astype(ml_dtypes.bfloat16)
    low = (table - high.astype(np.float64)).astype(np.float32).astype(ml_dtypes.bfloat16)
    return np.stack([high, low])


def class_of():
    d = np.arange(LEN)
    rest = np.where(d == 0, 64, 128 - d)
    third = np.where(d == 0, 32, 64 - d)
    fourth = np.where(d == 0, 96, 64 + d)
    return np.stack([d, rest, third, fourth], axis=1)


@functools.lru_cache(None)
def tables():
    turn = 2.0 * math.pi
    w_row = np.arange(ROWS)
    w = w_row // 16 + 8 * (w_row % 16)
    r = np.arange(ROWS)
    row_tables = []
    for a in range(4):
        angle = turn * ((w[:, None] * r[None, :] % 128) / 128.0 + a * r[None, :] / 512.0)
        cos, sin = np.cos(angle), np.sin(angle)
        row_tables.append(halves(np.block([[cos, -sin], [sin, cos]])))
    row_dft = np.stack(row_tables)
    lane = np.arange(LANES)
    e, m = lane // 8, lane % 8
    same = (m[:, None] == m[None, :]).astype(np.float64)
    angle = turn * (e[:, None] * e[None, :] % 16) / 16.0
    cos, sin = 0.5 * same * np.cos(angle), 0.5 * same * np.sin(angle)
    lane_dft = halves(np.block([[cos, sin], [-sin, cos]]))
    v = np.arange(128)
    c = class_of().reshape(-1)
    angle = turn * (v[:, None] * c[None, :] % 128) / 128.0
    cos, sin = np.cos(angle), np.sin(angle)
    class_dft = halves(np.block([[cos, -sin], [sin, cos]]))
    upper = np.arange(4)[:, None] + 4 * w[None, :]
    angle = turn * (upper.reshape(-1)[:, None] * e[None, :]) / 8192.0
    twist = np.stack([np.cos(angle), np.sin(angle)]).astype(np.float32)
    fold = np.zeros((512, 32), np.float32)
    index = np.arange(512)
    fold[index, 8 * (index // 128) + index % 8] = 1.0
    return row_dft, lane_dft, class_dft, twist, fold, upper.reshape(-1)


@functools.lru_cache(None)
def sine_terms():
    h = np.cos(np.pi * (np.arange(4000) + 0.5) / 4000) * 1.575
    z = h * h
    sin = np.linalg.lstsq(np.stack([h ** (2 * n + 1) for n in range(6)], 1), np.sin(h), rcond=None)[0]
    cos = np.linalg.lstsq(np.stack([z**n for n in range(1, 7)], 1), np.cos(h) - 1.0, rcond=None)[0]
    return [float(x) for x in sin], [float(x) for x in cos]


def cos_sin(phase):
    sin_terms, cos_terms = sine_terms()
    half = phase * 0.5
    z = half * half
    s = jnp.full_like(z, sin_terms[-1])
    for term in sin_terms[-2::-1]:
        s = s * z + term
    s = s * half
    c = jnp.full_like(z, cos_terms[-1])
    for term in cos_terms[-2::-1]:
        c = c * z + term
    c = c * z + 1.0
    return 1.0 - 2.0 * (s * s), 2.0 * (s * c)


def split(x):
    high = x.astype(BF16)
    return high, (x - high.astype(F32)).astype(BF16)


def dot(a, b):
    return jnp.dot(a, b, preferred_element_type=F32)


def sort_kernel(left_ref, right_ref, out_ref):
    for index, ref in enumerate((left_ref, right_ref)):

        def step(i, carry, index=index, ref=ref):
            tiles = [ref[:, pl.ds(pl.multiple_of(i * 2048 + e * 128, 128), 128)] for e in range(16)]
            block = jnp.concatenate(tiles, axis=0)
            out_ref[pl.ds(index * 16 + i, 128, stride=32), :] = block.T
            return carry

        lax.fori_loop(0, 16, step, 0)


def sort_phases(left, right):
    return pl.pallas_call(
        sort_kernel,
        out_shape=jax.ShapeDtypeStruct((4096, LANES), F32),
        compiler_params=pltpu.CompilerParams(vmem_limit_bytes=VMEM_LIMIT),
        name="sort_phases",
    )(left, right)


def meet(partners):
    barrier = pltpu.get_barrier_semaphore()
    total = 0
    for axis, size in partners:
        me = lax.axis_index(axis)

        def greet(r, carry, axis=axis, size=size, me=me):
            pl.semaphore_signal(barrier, inc=1, device_id={axis: lax.rem(me + r, size)}, device_id_type=MESH)
            return carry

        lax.fori_loop(1, size, greet, 0)
        total += size - 1
    pl.semaphore_wait(barrier, total)


def exchange1_kernel(src, dst, send, recv, own):
    me = lax.axis_index("len")
    meet([("len", LEN)])

    def classes(d):
        first = d == 0
        return (d, jnp.where(first, 64, 128 - d), jnp.where(first, 32, 64 - d), jnp.where(first, 96, 64 + d))

    mine = [pltpu.make_async_copy(src.at[c], dst.at[me, slot], own.at[slot]) for slot, c in enumerate(classes(me))]
    for copy in mine:
        copy.start()

    def start(r, carry):
        d = lax.rem(me + r, LEN)
        for slot, c in enumerate(classes(d)):
            pltpu.make_async_remote_copy(
                src.at[c], dst.at[me, slot], send.at[r], recv.at[r], device_id={"len": d}, device_id_type=MESH
            ).start()
        return carry

    lax.fori_loop(1, LEN, start, 0)
    for copy in mine:
        copy.wait()

    def finish(r, carry):
        source = lax.rem(me + LEN - r, LEN)
        whole = pltpu.make_async_remote_copy(
            dst.at[source], dst.at[source], send.at[r], recv.at[r], device_id={"len": source}, device_id_type=MESH
        )
        whole.wait_send()
        whole.wait_recv()
        return carry

    lax.fori_loop(1, LEN, finish, 0)


def exchange1(sorted_phases):
    return pl.pallas_call(
        exchange1_kernel,
        out_shape=jax.ShapeDtypeStruct((LEN, 4, 32, LANES), F32),
        in_specs=[pl.BlockSpec(memory_space=pl.ANY)],
        out_specs=pl.BlockSpec(memory_space=pl.ANY),
        scratch_shapes=[
            pltpu.SemaphoreType.DMA((LEN,)),
            pltpu.SemaphoreType.DMA((LEN,)),
            pltpu.SemaphoreType.DMA((4,)),
        ],
        compiler_params=pltpu.CompilerParams(collective_id=0, has_side_effects=True),
        name="exchange_phases",
    )(sorted_phases)


def exchange_kernel(with_mem, src, *refs):
    if with_mem:
        dst, dst_mem, send, recv, own, send_mem, recv_mem, own_mem = refs
    else:
        dst, send, recv, own = refs
    me = lax.axis_index("len")
    meet([("len", LEN), ("mem", MEM)] if with_mem else [("len", LEN)])
    mine = [pltpu.make_async_copy(src.at[me], dst.at[me], own)]
    if with_mem:
        my_mem = lax.axis_index("mem")
        quarter = LEN // MEM
        mine.append(pltpu.make_async_copy(src.at[pl.ds(my_mem * quarter, quarter)], dst_mem.at[my_mem], own_mem))
    for copy in mine:
        copy.start()

    def start(r, carry):
        d = lax.rem(me + r, LEN)
        pltpu.make_async_remote_copy(
            src.at[d], dst.at[me], send.at[r], recv.at[r], device_id={"len": d}, device_id_type=MESH
        ).start()
        return carry

    lax.fori_loop(1, LEN, start, 0)
    if with_mem:

        def start_mem(r, carry):
            d = lax.rem(my_mem + r, MEM)
            pltpu.make_async_remote_copy(
                src.at[pl.ds(d * quarter, quarter)],
                dst_mem.at[my_mem],
                send_mem.at[r],
                recv_mem.at[r],
                device_id={"mem": d},
                device_id_type=MESH,
            ).start()
            return carry

        lax.fori_loop(1, MEM, start_mem, 0)
    for copy in mine:
        copy.wait()

    def finish(r, carry):
        source = lax.rem(me + LEN - r, LEN)
        whole = pltpu.make_async_remote_copy(
            dst.at[source], dst.at[source], send.at[r], recv.at[r], device_id={"len": source}, device_id_type=MESH
        )
        whole.wait_send()
        whole.wait_recv()
        return carry

    lax.fori_loop(1, LEN, finish, 0)
    if with_mem:

        def finish_mem(r, carry):
            source = lax.rem(my_mem + MEM - r, MEM)
            whole = pltpu.make_async_remote_copy(
                dst_mem.at[source],
                dst_mem.at[source],
                send_mem.at[r],
                recv_mem.at[r],
                device_id={"mem": source},
                device_id_type=MESH,
            )
            whole.wait_send()
            whole.wait_recv()
            return carry

        lax.fori_loop(1, MEM, finish_mem, 0)


def exchange(blocks, collective, with_mem):
    blocks = blocks.reshape(LEN, ROWS, LANES)
    out_shape = [jax.ShapeDtypeStruct((LEN, ROWS, LANES), F32)]
    scratch = [pltpu.SemaphoreType.DMA((LEN,)), pltpu.SemaphoreType.DMA((LEN,)), pltpu.SemaphoreType.DMA]
    if with_mem:
        out_shape.append(jax.ShapeDtypeStruct((MEM, LEN // MEM, ROWS, LANES), F32))
        scratch += [pltpu.SemaphoreType.DMA((MEM,)), pltpu.SemaphoreType.DMA((MEM,)), pltpu.SemaphoreType.DMA]
    return pl.pallas_call(
        functools.partial(exchange_kernel, with_mem),
        out_shape=out_shape,
        in_specs=[pl.BlockSpec(memory_space=pl.ANY)],
        out_specs=[pl.BlockSpec(memory_space=pl.ANY)] * len(out_shape),
        scratch_shapes=scratch,
        compiler_params=pltpu.CompilerParams(collective_id=collective, has_side_effects=True),
        name="exchange_%d" % collective,
    )(blocks)


def partial_kernel(
    slots_ref, phases_ref, member_ref, column_ref, turn_ref, row_ref, lane_ref, twist_ref, out_ref, high_ref, low_ref, part_ref
):
    level = member_ref[0:1, :]
    exponent = member_ref[1:2, :]
    inverse = member_ref[2:3, :]

    def spectra(index, carry):
        slot = lax.div(index, 8)
        low_p = lax.rem(index, 8)
        row = lax.broadcasted_iota(jnp.int32, (16, LANES), 0)
        lane = lax.broadcasted_iota(jnp.int32, (16, LANES), 1)
        offset = row * 2048 + lax.div(lane, 8) * 128 + slots_ref[slot]
        parts = []
        for q in range(4):
            p = 8 * q + low_p
            freq = (offset + p * 32768).astype(F32)
            amplitude = level * jnp.exp(exponent * jnp.log(freq * (1.0 / ANCHOR) + 1.0))
            ratio = freq * inverse
            square = ratio * ratio
            coherent = 1.0 / (1.0 + square)
            incoherent = ratio * jnp.sqrt(2.0 + square) * coherent
            cos_left, sin_left = cos_sin(phases_ref[p, slot, 0:16, :])
            cos_right, sin_right = cos_sin(phases_ref[p, slot, 16:32, :])
            first, second = amplitude * coherent, amplitude * incoherent
            parts.append(
                (
                    amplitude * cos_left,
                    amplitude * sin_left,
                    first * cos_left + second * cos_right,
                    first * sin_left + second * sin_right,
                )
            )
        rows = pl.ds(pl.multiple_of(low_p * 16, 16), 16)
        imag_rows = pl.ds(pl.multiple_of(128 + low_p * 16, 16), 16)
        for track in range(2):
            re = [part[2 * track] for part in parts]
            im = [part[2 * track + 1] for part in parts]
            even_re, even_im = re[0] + re[2], im[0] + im[2]
            odd_re, odd_im = re[1] + re[3], im[1] + im[3]
            diff_re, diff_im = re[0] - re[2], im[0] - im[2]
            skew_re, skew_im = re[1] - re[3], im[1] - im[3]
            results = (
                (even_re + odd_re, even_im + odd_im),
                (diff_re - skew_im, diff_im + skew_re),
                (even_re - odd_re, even_im - odd_im),
                (diff_re + skew_im, diff_im - skew_re),
            )
            lanes = slice(track * 128, track * 128 + 128)
            for a, (x, y) in enumerate(results):
                high, low = split(x)
                high_ref[a, slot, rows, lanes] = high
                low_ref[a, slot, rows, lanes] = low
                high, low = split(y)
                high_ref[a, slot, imag_rows, lanes] = high
                low_ref[a, slot, imag_rows, lanes] = low
        return carry

    lax.fori_loop(0, 32, spectra, 0)
    is_first = slots_ref[0] == 0

    def transform(a, carry):
        table_high, table_low = row_ref[a, 0], row_ref[a, 1]
        twist_cos, twist_sin = twist_ref[0, a], twist_ref[1, a]
        for slot in range(4):
            high, low = high_ref[a, slot], low_ref[a, slot]
            partial = dot(table_high, high) + dot(table_low, high) + dot(table_high, low)
            column_cos = column_ref[a, :, 2 * slot : 2 * slot + 1]
            column_sin = column_ref[a, :, 2 * slot + 1 : 2 * slot + 2]
            cos = twist_cos * column_cos - twist_sin * column_sin
            sin = twist_cos * column_sin + twist_sin * column_cos
            stacked = []
            for track in range(2):
                re = partial[:128, track * 128 : track * 128 + 128]
                im = partial[128:, track * 128 : track * 128 + 128]
                stacked.append(jnp.concatenate([re * cos - im * sin, re * sin + im * cos], axis=1))
            high, low = split(jnp.concatenate(stacked, axis=0))
            done = dot(high, lane_ref[0]) + dot(low, lane_ref[0]) + dot(high, lane_ref[1])
            cos, sin = turn_ref[2 * slot : 2 * slot + 1, :], turn_ref[2 * slot + 1 : 2 * slot + 2, :]
            re, im = done[:, :128], done[:, 128:]
            part_ref[slot, 0] = re * cos - im * sin
            part_ref[slot, 1] = re * sin + im * cos
        for slot in (0, 2):
            re0, im0 = part_ref[slot, 0, :128, :], part_ref[slot, 1, :128, :]
            re1, im1 = part_ref[slot, 0, 128:, :], part_ref[slot, 1, 128:, :]
            mirror_re0, mirror_im0 = part_ref[slot + 1, 0, :128, :], part_ref[slot + 1, 1, :128, :]
            mirror_re1, mirror_im1 = part_ref[slot + 1, 0, 128:, :], part_ref[slot + 1, 1, 128:, :]
            sum_re0, sum_re1 = re0 + mirror_re0, re1 + mirror_re1
            gap_im0, gap_im1 = im0 - mirror_im0, im1 - mirror_im1
            pair = [
                [sum_re0 - gap_im1, gap_im0 + sum_re1],
                [sum_re0 + gap_im1, sum_re1 - gap_im0],
            ]
            if slot == 0:
                alone = [[re0 + re0, re1 + re1], [mirror_re0 + mirror_re0, mirror_re1 + mirror_re1]]
                pair = [[jnp.where(is_first, alone[n][x], pair[n][x]) for x in range(2)] for n in range(2)]
            for n in range(2):
                for x in range(2):
                    out_ref[:, a, slot + n, x] = pair[n][x].reshape(8, 16, LANES)
        return carry

    lax.fori_loop(0, 4, transform, 0)


def partial_transforms(slots, phases, member_rows, columns, turns):
    row_dft, lane_dft, _, twist, _, _ = tables()
    smem = pl.BlockSpec(memory_space=pltpu.SMEM)
    vmem = pl.BlockSpec(memory_space=pltpu.VMEM)
    return pl.pallas_call(
        partial_kernel,
        out_shape=jax.ShapeDtypeStruct((8, 4, 4, 2, 16, LANES), F32),
        in_specs=[smem] + [vmem] * 7,
        out_specs=vmem,
        scratch_shapes=[
            pltpu.VMEM((4, 4, 256, 256), BF16),
            pltpu.VMEM((4, 4, 256, 256), BF16),
            pltpu.VMEM((4, 2, 256, LANES), F32),
        ],
        compiler_params=pltpu.CompilerParams(vmem_limit_bytes=VMEM_LIMIT),
        name="partial_transforms",
    )(
        slots,
        phases,
        member_rows,
        columns,
        turns,
        jnp.asarray(row_dft),
        jnp.asarray(lane_dft),
        jnp.asarray(twist.reshape(2, 4, ROWS, LANES)),
    )


def gram_kernel(blocks_ref, fold_ref, out_ref, total_ref):
    total_ref[...] = jnp.zeros_like(total_ref)
    contract = (((0,), (0,)), ((), ()))

    def step(n, carry):
        rows = [blocks_ref[z, pl.ds(pl.multiple_of(n * 256, 256), 256), :] for z in range(MEM)]
        high, low = split(jnp.concatenate(rows, axis=1))
        product = functools.partial(lax.dot_general, dimension_numbers=contract, preferred_element_type=F32)
        total_ref[...] += product(high, high) + product(low, high) + product(high, low)
        return carry

    lax.fori_loop(0, 4, step, 0)
    row = lax.broadcasted_iota(jnp.int32, (512, 512), 0)
    column = lax.broadcasted_iota(jnp.int32, (512, 512), 1)
    same = lax.rem(lax.div(row, 8), 16) == lax.rem(lax.div(column, 8), 16)
    kept = jnp.where(same, total_ref[...], 0.0)
    exact = functools.partial(jnp.dot, preferred_element_type=F32, precision=lax.Precision.HIGHEST)
    right = exact(kept, fold_ref[...])
    out_ref[...] = exact(fold_ref[...].T, right) * (128.0 / (2.0 * POINTS))


def gram_part(blocks):
    return pl.pallas_call(
        gram_kernel,
        out_shape=jax.ShapeDtypeStruct((32, 32), F32),
        scratch_shapes=[pltpu.VMEM((512, 512), F32)],
        compiler_params=pltpu.CompilerParams(vmem_limit_bytes=VMEM_LIMIT),
        name="gram_part",
    )(blocks.reshape(MEM, 1024, LANES), jnp.asarray(tables()[4]))


def class_kernel(blocks_ref, table_ref, out_ref):
    def step(n, carry):
        columns = []
        for u2 in (2 * n, 2 * n + 1):
            re = blocks_ref[pl.ds(u2, 128, stride=32), :]
            im = blocks_ref[pl.ds(16 + u2, 128, stride=32), :]
            columns.append(jnp.concatenate([re, im], axis=0))
        high, low = split(jnp.concatenate(columns, axis=1))
        done = dot(table_ref[0], high) + dot(table_ref[1], high) + dot(table_ref[0], low)
        for index in range(2):
            for track in range(2):
                out_ref[pl.ds(16 * track + 2 * n + index, 128, stride=32), :] = done[
                    track * 128 : track * 128 + 128, index * 128 : index * 128 + 128
                ]
        return carry

    lax.fori_loop(0, 8, step, 0)


def class_transform(blocks):
    return pl.pallas_call(
        class_kernel,
        out_shape=jax.ShapeDtypeStruct((4096, LANES), F32),
        compiler_params=pltpu.CompilerParams(vmem_limit_bytes=VMEM_LIMIT),
        name="class_transform",
    )(blocks.reshape(4096, LANES), jnp.asarray(tables()[2]))


def place_kernel(blocks_ref, out_ref):
    def step(index, carry):
        vl = lax.div(index, 8)
        track = lax.rem(lax.div(index, 4), 2)
        high_u2 = lax.rem(index, 4)
        base = vl * 32 + track * 16 + high_u2 * 4
        rows = [blocks_ref[pl.ds(base + low, 32, stride=128), :] for low in range(4)]
        turned = jnp.concatenate(rows, axis=0).T
        for u3 in range(16):
            column = pl.multiple_of((vl * 64 + u3 * 4 + high_u2) * 128, 128)
            out_ref[track, :, pl.ds(column, 128)] = turned[8 * u3 : 8 * u3 + 8, :]
        return carry

    lax.fori_loop(0, 32, step, 0)


def place(blocks):
    return pl.pallas_call(
        place_kernel,
        out_shape=jax.ShapeDtypeStruct((2, 8, 32768), F32),
        compiler_params=pltpu.CompilerParams(vmem_limit_bytes=VMEM_LIMIT),
        name="place_profile",
    )(blocks.reshape(4096, LANES))


def device_tables(me):
    upper = tables()[5]
    first = me == 0
    slots = jnp.stack(
        [me, jnp.where(first, 64, 128 - me), jnp.where(first, 32, 64 - me), jnp.where(first, 96, 64 + me)]
    ).astype(jnp.int32)
    turn = 2.0 * math.pi
    angle = (jnp.asarray(upper, jnp.int32)[:, None] * slots[None, :]).astype(F32) * (turn / POINTS)
    columns = jnp.stack([jnp.cos(angle), jnp.sin(angle)], axis=2).reshape(4, ROWS, 8)
    angle = (jnp.asarray(np.arange(LANES) // 8, jnp.int32)[None, :] * slots[:, None]).astype(F32) * (turn / 2048)
    turns = jnp.stack([jnp.cos(angle), jnp.sin(angle)], axis=1).reshape(8, LANES)
    return slots, columns, turns


def per_device(phase_left, phase_right, roughness, waviness, coherence):
    me = lax.axis_index("len")
    slots, columns, turns = device_tables(me)
    level = jnp.sqrt(2.0 * roughness * (waviness - 1.0) / ANCHOR)
    member_rows = jnp.tile(jnp.stack([level, -0.5 * waviness, 1.0 / coherence]), (1, 16))
    sorted_phases = sort_phases(phase_left, phase_right)
    phases = exchange1(sorted_phases.reshape(128, 32, LANES))
    partial = partial_transforms(slots, phases, member_rows, columns, turns)
    blocks, members = exchange(partial, 1, True)
    gram = lax.psum(gram_part(members), ("len", "mem"))
    outgoing = class_transform(blocks)
    (arrived,) = exchange(outgoing, 2, False)
    profile = place(arrived)
    r_factor = jnp.linalg.cholesky(gram).T
    return profile, r_factor


def solution(mesh):
    placed = (P("mem", "len"), P("mem", "len"), P("mem"), P("mem"), P("mem"))
    return jax.shard_map(
        per_device,
        mesh=mesh,
        in_specs=placed,
        out_specs=(P(None, "mem", "len"), P()),
        check_vma=False,
    )
```

time: 596 us -> 248 us (0.42); the launches traced: 587 us -> 248 us
  matrix products: 190 us -> 0 us
  Pallas kernels: 0 us -> 165 us
  other arithmetic: 153 us -> 6.64 us
  local copies, waits for them, and re-layouts: 102 us -> 3.72 us
  waiting for transfers between devices: 42.5 us -> 0 us
  starting transfers between devices: 26 us -> 0 us
  between operations: 14.5 us -> 0.72 us
  blocking collectives: 58.7 us -> 71.4 us
    dot_general x69 -> x0, matrix products: 190 us -> none  [the longest x1 35.5 us: per_device(): first = jnp.einsum('jqa,qiac->cij', outer_cos, real_in, precision=highest)]
    pallas_call x0 -> x8, Pallas kernels: none -> 165 us  [the longest x2 82.7 us: exchange(): pl.pallas_call(functools.partial(exchange_kernel, with_mem), out_shape=ou...]
    another operation x96 -> x8, other arithmetic: 115 us -> 4.4 us  [the longest x3 3.59 us: per_device(): r_factor = jnp.linalg.cholesky(gram).T]
    psum x0 -> x1, blocking collectives: none -> 71.4 us  [per_device(): gram = lax.psum(gram_part(members), ('len', 'mem'))]
    reshape x8 -> x2, local copies, waits for them, and re-layouts: 46.2 us -> 0.89 us  [device_tables(): jnp.stack([jnp.cos(angle), jnp.sin(angle)], axis=2).reshape(4, ROWS, 8)]
    all_to_all x4 -> x0, waiting for transfers between devices: 42.5 us -> none  [the longest x1 28.1 us: per_device(): lax.all_to_all(outgoing, 'len', split_axis=0, concat_axis=0, tiled=True)]
    all_to_all x1 -> x0, blocking collectives: 35.5 us -> none  [per_device(): lax.all_to_all(rot_imag, 'len', split_axis=0, concat_axis=0, tiled=True)]
    all_to_all x4 -> x0, starting transfers between devices: 26 us -> none  [the longest x1 8.77 us: per_device(): lax.all_to_all(to_rows(real_part), 'len', split_axis=1, concat_axis=0, ti...]
  transfers between devices with their start and end apart: 5 -> 0, of which waited for: 2 -> 0; matrix products, arithmetic and copies ran while one was open for 22% -> 0% of each run, Pallas kernels for 0% -> 0%
where the time goes in v1:
time: 248 us
  Pallas kernels  165 us (67%)
  blocking collectives  71.4 us (29%)
  other arithmetic  6.64 us (3%)
  local copies, waits for them, and re-layouts  3.72 us (2%)
    pallas_call x2, Pallas kernels, exchange(): pl.pallas_call(functools.partial(exchange_kernel, with_mem), out_shape=ou...  82.7 us
    psum x1, blocking collectives, per_device(): gram = lax.psum(gram_part(members), ('len', 'mem'))  71.4 us
    pallas_call x1, Pallas kernels, exchange1(): pl.pallas_call(exchange1_kernel, out_shape=jax.ShapeDtypeStruct((LEN, 4,...  42.3 us
    pallas_call x1, Pallas kernels, partial_transforms(): pl.pallas_call(partial_kernel, out_shape=jax.ShapeDtypeStruct((8, 4, 4, 2...  13.6 us
    pallas_call x1, Pallas kernels, sort_phases(): pl.pallas_call(sort_kernel, out_shape=jax.ShapeDtypeStruct((4096, LANES),...  7.12 us
    pallas_call x1, Pallas kernels, class_transform(): pl.pallas_call(class_kernel, out_shape=jax.ShapeDtypeStruct((4096, LANES)...  7.09 us
    pallas_call x1, Pallas kernels, place(): pl.pallas_call(place_kernel, out_shape=jax.ShapeDtypeStruct((2, 8, 32768)...  6.5 us
    pallas_call x1, Pallas kernels, gram_part(): pl.pallas_call(gram_kernel, out_shape=jax.ShapeDtypeStruct((32, 32), F32)...  6.08 us

profile of v1, /device:TPU:1, one launch (start us, length us, event | category | flops | bytes accessed | tf_op | source)
XLA Modules:
  0.0 247.8 jit_solution(11274758863792292397)
XLA Ops:
  0.6 0.1 pad_add_fusion.slots_ref
  0.7 0.0 copy-start
  0.7 0.7 sqrt_bitcast_fusion
  1.4 0.8 fusion.4
  2.2 0.6 copy.22
  2.8 0.8 fusion.2
  3.7 0.7 tile.10.member_ref
  4.4 0.9 copy.23.column_ref
  5.3 7.1 %sort_phases.1 = f32[4096,128]{1,0:T(8,128)} custom-call(f32[8,32768]{1,0:T(8,128)} %left_ref.1, f32[8,32768]{1,0:T(8,128)} %right_ref.1), custom_call_target="tpu_custom_call" | custom-call | tf_op jit(solution)/shard_map/sort_phases/pallas_call | solution.py:118
  12.4 0.0 copy-done
  12.4 42.3 %exchange_phases.1.phases_ref = f32[32,4,32,128]{3,2,1,0:T(8,128)} custom-call(f32[128,32,128]{2,1,0:T(8,128)} %bitcast.28), custom_call_target="tpu_custom_call" | custom-call | tf_op jit(solution)/shard_map/exchange_phases/pallas_call | solution.py:178
  54.7 13.6 %partial_transforms.1 = f32[8,4,4,2,16,128]{5,4,3,2,1,0:T(8,128)} custom-call(s32[4]{0:T(128)} %copy-done, f32[32,4,32,128]{3,2,1,0:T(8,128)} %exchange_phases.1.phases_ref, f32[3,128]{1,0:T(4,128)} %tile.10.member_ref, f32[4,128,8]{2,1,0:T(8,128)} %copy.23.column_ref, f32[8,128]{1,0:T(8,128)} %bitcast.31, bf16[4,2,256,256]{3,2,1,0:T(8,128)(2,1)} %constant.84.clone.row_ref, ...), custom_call_target="tpu_custom_call" | custom-call | tf_op jit(solution)/shard_map/partial_transforms/pallas_call | solution.py:389
  68.2 42.9 %exchange_1.1 = (f32[32,128,128]{2,1,0:T(8,128)}, f32[4,8,128,128]{3,2,1,0:T(8,128)}) custom-call(f32[32,128,128]{2,1,0:T(8,128)} %bitcast.25), custom_call_target="tpu_custom_call" | custom-call | tf_op jit(solution)/shard_map/exchange_1/pallas_call | solution.py:270
  111.1 7.1 %class_transform.1 = f32[4096,128]{1,0:T(8,128)} custom-call(f32[4096,128]{1,0:T(8,128)} %bitcast.30, bf16[2,256,256]{2,1,0:T(8,128)(2,1)} %constant.88.clone.table_ref), custom_call_target="tpu_custom_call" | custom-call | tf_op jit(solution)/shard_map/class_transform/pallas_call | solution.py:464
  118.2 39.8 %exchange_2.1 = f32[32,128,128]{2,1,0:T(8,128)} custom-call(f32[32,128,128]{2,1,0:T(8,128)} %bitcast.26), custom_call_target="tpu_custom_call" | custom-call | tf_op jit(solution)/shard_map/exchange_2/pallas_call | solution.py:270
  158.0 6.5 %place_profile.1 = f32[2,8,32768]{2,1,0:T(8,128)} custom-call(f32[4096,128]{1,0:T(8,128)} %bitcast.27), custom_call_target="tpu_custom_call" | custom-call | tf_op jit(solution)/shard_map/place_profile/pallas_call | solution.py:489
  164.5 6.1 %gram_part.1 = f32[32,32]{1,0:T(8,128)} custom-call(f32[4,1024,128]{2,1,0:T(8,128)} %bitcast.29, f32[512,32]{1,0:T(8,128)} %constant.87.clone.fold_ref), custom_call_target="tpu_custom_call" | custom-call | tf_op jit(solution)/shard_map/gram_part/pallas_call | solution.py:435
  170.6 0.8 copy.24
  171.4 71.4 %psum.7 = f32[32,32]{0,1:T(8,128)S(1)} all-reduce(f32[32,32]{0,1:T(8,128)S(1)} %copy.24), channel_id=1, replica_groups=mesh['len'=32,'mem'=4] {'len','mem'}, use_global_device_ids=true, to_apply=%region_0.1 | all-reduce | flops 1024 | bytes 8192 | tf_op jit(solution)/shard_map/psum | solution.py:520
  242.8 0.1 copy.25
  242.9 2.9 %cholesky.18 = f32[32,32]{1,0:T(8,128)S(1)} custom-call(f32[32,32]{1,0:T(8,128)S(1)} %fusion), custom_call_target="Cholesky" | custom-call | tf_op jit(solution)/shard_map/jit(cholesky)/cholesky | solution.py:524
  245.8 0.6 compare_reduce_fusion
  246.5 0.6 select_bitcast_fusion
  247.1 0.7 copy.26
  (8 shorter events, 0.1 us)
Async XLA Ops:
  0.7 11.7 %copy-start = (s32[4]{0:T(128)}, s32[4]{0:T(128)S(1)}, u32[]{:S(2)}) copy-start(s32[4]{0:T(128)S(1)} %pad_add_fusion.slots_ref) | copy-start | bytes 52

commit v2 on v0

v2 whole, which is shorter than its diff:
```python
import functools
import math

import jax
import jax.numpy as jnp
import ml_dtypes
import numpy as np
from jax import lax
from jax.experimental import pallas as pl
from jax.experimental.pallas import tpu as pltpu
from jax.sharding import PartitionSpec as P

ANCHOR = 64
POINTS = 1048576
LEN = 32
MEM = 4
ROWS = 128
LANES = 128
F32 = jnp.float32
BF16 = jnp.bfloat16
MESH = pl.DeviceIdType.MESH
VMEM_LIMIT = 56 * 1024 * 1024


def halves(table):
    table = np.asarray(table, np.float64)
    high = table.astype(np.float32).astype(ml_dtypes.bfloat16)
    low = (table - high.astype(np.float64)).astype(np.float32).astype(ml_dtypes.bfloat16)
    return np.stack([high, low])


def class_of():
    d = np.arange(LEN)
    rest = np.where(d == 0, 64, 128 - d)
    third = np.where(d == 0, 32, 64 - d)
    fourth = np.where(d == 0, 96, 64 + d)
    return np.stack([d, rest, third, fourth], axis=1)


@functools.lru_cache(None)
def tables():
    turn = 2.0 * math.pi
    w_row = np.arange(ROWS)
    w = w_row // 16 + 8 * (w_row % 16)
    r = np.arange(ROWS)
    row_tables = []
    for a in range(4):
        angle = turn * ((w[:, None] * r[None, :] % 128) / 128.0 + a * r[None, :] / 512.0)
        cos, sin = np.cos(angle), np.sin(angle)
        row_tables.append(halves(np.block([[cos, -sin], [sin, cos]])))
    row_dft = np.stack(row_tables)
    lane = np.arange(LANES)
    e, m = lane // 8, lane % 8
    same = (m[:, None] == m[None, :]).astype(np.float64)
    angle = turn * (e[:, None] * e[None, :] % 16) / 16.0
    cos, sin = 0.5 * same * np.cos(angle), 0.5 * same * np.sin(angle)
    lane_dft = halves(np.block([[cos, sin], [-sin, cos]]))
    v = np.arange(128)
    c = class_of().reshape(-1)
    angle = turn * (v[:, None] * c[None, :] % 128) / 128.0
    cos, sin = np.cos(angle), np.sin(angle)
    class_dft = halves(np.block([[cos, -sin], [sin, cos]]))
    index = np.arange(512)
    fold = np.zeros((512, LANES), np.float32)
    for a in range(4):
        fold[index, 32 * a + 8 * (index // 128) + index % 8] = 1.0
    return row_dft, lane_dft, class_dft, fold


@functools.lru_cache(None)
def sine_terms():
    h = np.cos(np.pi * (np.arange(4000) + 0.5) / 4000) * 1.575
    z = h * h
    sin = np.linalg.lstsq(np.stack([h ** (2 * n + 1) for n in range(6)], 1), np.sin(h), rcond=None)[0]
    cos = np.linalg.lstsq(np.stack([z**n for n in range(1, 7)], 1), np.cos(h) - 1.0, rcond=None)[0]
    return [float(x) for x in sin], [float(x) for x in cos]


def cos_sin(phase):
    sin_terms, cos_terms = sine_terms()
    half = phase * 0.5
    z = half * half
    s = jnp.full_like(z, sin_terms[-1])
    for term in sin_terms[-2::-1]:
        s = s * z + term
    s = s * half
    c = jnp.full_like(z, cos_terms[-1])
    for term in cos_terms[-2::-1]:
        c = c * z + term
    c = c * z + 1.0
    return 1.0 - 2.0 * (s * s), 2.0 * (s * c)


def split(x):
    high = x.astype(BF16)
    return high, (x - high.astype(F32)).astype(BF16)


def dot(a, b):
    return jnp.dot(a, b, preferred_element_type=F32)


def order():
    ring = lambda n: min(n, 4 - n)
    steps = [(dx, dy, dc) for dc in range(2) for dx in range(4) for dy in range(4) if (dx, dy, dc) != (0, 0, 0)]
    return sorted(steps, key=lambda s: (-ring(s[0]) - ring(s[1]), s[2]))


def partners(me):
    x, y, core = lax.div(me, 8), lax.rem(lax.div(me, 2), 4), lax.rem(me, 2)
    for dx, dy, dc in order():
        yield lax.rem(x + dx, 4) * 8 + lax.rem(y + dy, 4) * 2 + lax.rem(core + dc, 2)


def classes(d):
    first = d == 0
    return (d, jnp.where(first, 64, 128 - d), jnp.where(first, 32, 64 - d), jnp.where(first, 96, 64 + d))


def rows_at(start, size):
    return pl.ds(pl.multiple_of(start, 8), size)


def send(source, target, sems, index, device):
    pltpu.make_async_remote_copy(
        source, target, sems.at[0, index], sems.at[1, index], device_id=device, device_id_type=MESH
    ).start()


def settle(ref, sems, index, device, which):
    copy = pltpu.make_async_remote_copy(
        ref, ref, sems.at[0, index], sems.at[1, index], device_id=device, device_id_type=MESH
    )
    if which == 0:
        copy.wait_send()
    else:
        copy.wait_recv()


def unit_turn(numerator, size):
    cos, sin = cos_sin(numerator.astype(F32) * (2.0 * math.pi / size) - math.pi)
    return -cos, -sin


def sort_phases(index, ref, sorted_ref):
    def step(i, carry):
        tiles = [ref[:, pl.ds(pl.multiple_of(i * 2048 + e * 128, 128), 128)] for e in range(16)]
        sorted_ref[pl.ds(index * 16 + i, 128, stride=32), :] = jnp.concatenate(tiles, axis=0).T
        return carry

    lax.fori_loop(0, 16, step, 0)


def member_lanes(ref):
    lane = lax.rem(lax.broadcasted_iota(jnp.int32, (8, LANES), 1), 8)
    values = jnp.zeros((8, LANES), F32)
    for m in range(8):
        values = jnp.where(lane == m, ref[m], values)
    return values


def fill_levels(pair, me, roughness_ref, waviness_ref, coherence_ref, level_ref):
    waviness = member_lanes(waviness_ref)
    scale = jnp.sqrt(2.0 * member_lanes(roughness_ref) * (waviness - 1.0) * (1.0 / ANCHOR))
    exponent = -0.5 * waviness
    inverse = 1.0 / member_lanes(coherence_ref)
    row = lax.broadcasted_iota(jnp.int32, (8, LANES), 0)
    lane = lax.broadcasted_iota(jnp.int32, (8, LANES), 1)
    spread = row * 2048 + lax.div(lane, 8) * 128
    for half in range(2):
        offset = spread + classes(me)[2 * pair + half]

        def step(n, carry, half=half, offset=offset):
            freq = (offset + n * 16384).astype(F32)
            amplitude = scale * jnp.exp(exponent * jnp.log(freq * (1.0 / ANCHOR) + 1.0))
            ratio = freq * inverse
            square = ratio * ratio
            coherent = 1.0 / (1.0 + square)
            incoherent = ratio * jnp.sqrt(2.0 + square) * coherent
            rows = rows_at(pair * 1024 + half * 512 + n * 8, 8)
            level_ref[0, rows, :] = amplitude
            level_ref[1, rows, :] = amplitude * coherent
            level_ref[2, rows, :] = amplitude * incoherent
            return carry

        lax.fori_loop(0, 64, step, 0, unroll=4)


def fill_twist(pair, me, twist_ref):
    row = lax.broadcasted_iota(jnp.int32, (8, LANES), 0)
    lane = lax.broadcasted_iota(jnp.int32, (8, LANES), 1)
    for half in range(2):
        place = lax.div(lane, 8) * 128 + classes(me)[2 * pair + half]

        def step(n, carry, half=half, place=place):
            upper = lax.div(n, 16) + 4 * lax.rem(lax.div(n, 2), 8) + 32 * (lax.rem(n, 2) * 8 + row)
            cos, sin = unit_turn(lax.rem(upper * place, POINTS), POINTS)
            rows = rows_at(pair * 1024 + half * 512 + n * 8, 8)
            twist_ref[0, rows, :] = cos
            twist_ref[1, rows, :] = sin
            return carry

        lax.fori_loop(0, 64, step, 0, unroll=4)


def spectra(pair, in_ref, level_ref, high_ref, low_ref):
    def step(index, carry):
        half = lax.div(index, 8)
        low_p = lax.rem(index, 8)
        parts = []
        for q in range(4):
            p = 8 * q + low_p
            start = pair * 2048 + p * 64 + half * 32
            cos_left, sin_left = cos_sin(in_ref[rows_at(start, 16), :])
            cos_right, sin_right = cos_sin(in_ref[rows_at(start + 16, 16), :])
            rows = rows_at(pair * 1024 + half * 512 + p * 16, 16)
            amplitude, first, second = level_ref[0, rows, :], level_ref[1, rows, :], level_ref[2, rows, :]
            parts.append(
                (
                    amplitude * cos_left,
                    amplitude * sin_left,
                    first * cos_left + second * cos_right,
                    first * sin_left + second * sin_right,
                )
            )
        rows = pl.ds(pl.multiple_of(low_p * 16, 16), 16)
        imag_rows = pl.ds(pl.multiple_of(128 + low_p * 16, 16), 16)
        for track in range(2):
            re = [part[2 * track] for part in parts]
            im = [part[2 * track + 1] for part in parts]
            even_re, even_im = re[0] + re[2], im[0] + im[2]
            odd_re, odd_im = re[1] + re[3], im[1] + im[3]
            diff_re, diff_im = re[0] - re[2], im[0] - im[2]
            skew_re, skew_im = re[1] - re[3], im[1] - im[3]
            results = (
                (even_re + odd_re, even_im + odd_im),
                (diff_re - skew_im, diff_im + skew_re),
                (even_re - odd_re, even_im - odd_im),
                (diff_re + skew_im, diff_im - skew_re),
            )
            lanes = slice(track * 128, track * 128 + 128)
            for a, (x, y) in enumerate(results):
                high, low = split(x)
                high_ref[a, half, rows, lanes] = high
                low_ref[a, half, rows, lanes] = low
                high, low = split(y)
                high_ref[a, half, imag_rows, lanes] = high
                low_ref[a, half, imag_rows, lanes] = low
        return carry

    lax.fori_loop(0, 16, step, 0)


def transforms(pair, me, high_ref, low_ref, row_ref, lane_ref, twist_ref, part_ref, out_ref):
    is_first = me == 0
    lane = lax.div(lax.broadcasted_iota(jnp.int32, (1, LANES), 1), 8)
    turns = [unit_turn(lane * classes(me)[2 * pair + half], 2048) for half in range(2)]

    def step(a, carry):
        table_high, table_low = row_ref[a, 0], row_ref[a, 1]
        for half in range(2):
            high, low = high_ref[a, half], low_ref[a, half]
            partial = dot(table_high, high) + dot(table_low, high) + dot(table_high, low)
            rows = pl.ds(pl.multiple_of(pair * 1024 + half * 512 + a * 128, 128), 128)
            cos, sin = twist_ref[0, rows, :], twist_ref[1, rows, :]
            stacked = []
            for track in range(2):
                re = partial[:128, track * 128 : track * 128 + 128]
                im = partial[128:, track * 128 : track * 128 + 128]
                stacked.append(jnp.concatenate([re * cos - im * sin, re * sin + im * cos], axis=1))
            high, low = split(jnp.concatenate(stacked, axis=0))
            done = dot(high, lane_ref[0]) + dot(low, lane_ref[0]) + dot(high, lane_ref[1])
            cos, sin = turns[half]
            re, im = done[:, :128], done[:, 128:]
            part_ref[half, 0] = re * cos - im * sin
            part_ref[half, 1] = re * sin + im * cos
        re0, im0 = part_ref[0, 0, :128, :], part_ref[0, 1, :128, :]
        re1, im1 = part_ref[0, 0, 128:, :], part_ref[0, 1, 128:, :]
        mirror_re0, mirror_im0 = part_ref[1, 0, :128, :], part_ref[1, 1, :128, :]
        mirror_re1, mirror_im1 = part_ref[1, 0, 128:, :], part_ref[1, 1, 128:, :]
        sum_re0, sum_re1 = re0 + mirror_re0, re1 + mirror_re1
        gap_im0, gap_im1 = im0 - mirror_im0, im1 - mirror_im1
        packed = [
            [sum_re0 - gap_im1, gap_im0 + sum_re1],
            [sum_re0 + gap_im1, sum_re1 - gap_im0],
        ]
        if pair == 0:
            alone = [[re0 + re0, re1 + re1], [mirror_re0 + mirror_re0, mirror_re1 + mirror_re1]]
            packed = [[jnp.where(is_first, alone[n][x], packed[n][x]) for x in range(2)] for n in range(2)]
        for n in range(2):
            for x in range(2):
                start = (2 * pair + n) * 32 + x * 16
                for wl in range(8):
                    out_ref[4 * wl + a, start : start + 16, :] = packed[n][x][wl * 16 : wl * 16 + 16, :]
        return carry

    lax.fori_loop(0, 4, step, 0)


def gram_part(members_ref, fold_ref, total_ref):
    total_ref[...] = jnp.zeros_like(total_ref)
    product = functools.partial(
        lax.dot_general, dimension_numbers=(((0,), (0,)), ((), ())), preferred_element_type=F32
    )

    def step(n, carry):
        rows = [members_ref[z, pl.ds(2 * n, 2)].reshape(256, LANES) for z in range(MEM)]
        high, low = split(jnp.concatenate(rows, axis=1))
        total_ref[...] += product(high, high) + product(low, high) + product(high, low)
        return carry

    lax.fori_loop(0, 4, step, 0)
    row = lax.broadcasted_iota(jnp.int32, (512, 512), 0)
    column = lax.broadcasted_iota(jnp.int32, (512, 512), 1)
    same = lax.rem(lax.div(row, 8), 16) == lax.rem(lax.div(column, 8), 16)
    kept = jnp.where(same, total_ref[...], 0.0)
    right = jnp.dot(kept, fold_ref[...], preferred_element_type=F32, precision=lax.Precision.HIGHEST)
    row = lax.broadcasted_iota(jnp.int32, (512, LANES), 0)
    lane = lax.broadcasted_iota(jnp.int32, (512, LANES), 1)
    right = jnp.where(lax.div(row, 128) == lax.div(lane, 32), right, 0.0)
    return jnp.sum(right.reshape(64, 8, LANES), axis=0) * (128.0 / (2.0 * POINTS))


def upper_factor(gram):
    row = lax.broadcasted_iota(jnp.int32, (32, LANES), 0)
    lane = lax.broadcasted_iota(jnp.int32, (32, LANES), 1)
    tall = jnp.concatenate([gram] * 4, axis=0)
    tall = jnp.where(lax.div(row, 8) == lax.div(lane, 32), tall, 0.0)
    pick_row = lax.broadcasted_iota(jnp.int32, (LANES, LANES), 0)
    pick_lane = lax.broadcasted_iota(jnp.int32, (LANES, LANES), 1)
    pick = jnp.where(lax.rem(pick_row, 32) == pick_lane, 1.0, 0.0)
    matrix = jnp.dot(tall, pick, preferred_element_type=F32, precision=lax.Precision.HIGHEST)

    def step(n, carry):
        rest, upper = carry
        line = jnp.sum(jnp.where(row == n, rest, 0.0), axis=0, keepdims=True)
        column = jnp.sum(jnp.where(lane == n, rest, 0.0), axis=1, keepdims=True)
        pivot = jnp.sum(jnp.where(lane[0:1] == n, line, 0.0), axis=1, keepdims=True)
        line = jnp.where(lane[0:1] >= n, line / jnp.sqrt(pivot), 0.0)
        column = column / jnp.sqrt(pivot)
        return rest - column * line, jnp.where(row == n, line, upper)

    return lax.fori_loop(0, 32, step, (matrix, jnp.zeros_like(matrix)))[1]


def class_transform(group, in_ref, table_ref, out_ref):
    def step(n, carry):
        columns = []
        for index in range(2):
            u2 = group * 8 + 2 * n + index
            re = in_ref[pl.ds(u2, 128, stride=32), :]
            im = in_ref[pl.ds(16 + u2, 128, stride=32), :]
            columns.append(jnp.concatenate([re, im], axis=0))
        high, low = split(jnp.concatenate(columns, axis=1))
        done = dot(table_ref[0], high) + dot(table_ref[1], high) + dot(table_ref[0], low)
        for index in range(2):
            for track in range(2):
                out_ref[pl.ds(group * 2048 + 8 * track + 2 * n + index, 128, stride=16), :] = done[
                    track * 128 : track * 128 + 128, index * 128 : index * 128 + 128
                ]
        return carry

    lax.fori_loop(0, 4, step, 0)


def place(group, in_ref, out_ref):
    def step(index, carry):
        vl = lax.div(index, 4)
        track = lax.rem(lax.div(index, 2), 2)
        high_u2 = lax.rem(index, 2)
        base = group * 2048 + vl * 16 + track * 8 + high_u2 * 4
        rows = [in_ref[pl.ds(base + low, 32, stride=64), :] for low in range(4)]
        turned = jnp.concatenate(rows, axis=0).T
        for u3 in range(16):
            column = pl.multiple_of((vl * 64 + u3 * 4 + group * 2 + high_u2) * 128, 128)
            out_ref[track, :, pl.ds(column, 128)] = turned[8 * u3 : 8 * u3 + 8, :]
        return carry

    lax.fori_loop(0, 16, step, 0)


def road_kernel(
    left_ref, right_ref, roughness_ref, waviness_ref, coherence_ref, row_hbm, lane_hbm, class_hbm, fold_hbm,
    profile_ref, factor_ref,
    row_ref, lane_ref, class_ref, fold_ref, sorted_ref, in1_ref, level_ref, twist_ref, high_ref, low_ref, part_ref,
    out2_ref, in2_ref, members_ref, total_ref, mine_ref, grams_ref, planes_ref, out3_ref, in3_ref,
    table_sem, own_sem, sems,
):
    me = lax.axis_index("len")
    plane = lax.axis_index("mem")
    other = {"len": lax.rem(me + 1, LEN)}
    above = {"mem": lax.rem(plane + 1, MEM)}
    loads = [
        pltpu.make_async_copy(source, target, table_sem.at[n])
        for n, (source, target) in enumerate(
            ((row_hbm, row_ref), (lane_hbm, lane_ref), (class_hbm, class_ref), (fold_hbm, fold_ref))
        )
    ]
    for load in loads:
        load.start()
    barrier = pltpu.get_barrier_semaphore()

    def greet(r, carry):
        pl.semaphore_signal(barrier, inc=1, device_id={"len": lax.rem(me + r, LEN)}, device_id_type=MESH)
        return carry

    lax.fori_loop(1, LEN, greet, 0)
    for r in range(1, MEM):
        pl.semaphore_signal(barrier, inc=1, device_id={"mem": lax.rem(plane + r, MEM)}, device_id_type=MESH)
    sort_phases(0, left_ref, sorted_ref)
    sort_phases(1, right_ref, sorted_ref)
    pl.semaphore_wait(barrier, LEN + MEM - 2)

    own = []
    for pair in range(2):
        for half in range(2):
            target = in1_ref.at[rows_at(pair * 2048 + me * 64 + half * 32, 32)]
            source = sorted_ref.at[rows_at(classes(me)[2 * pair + half] * 32, 32)]
            own.append(pltpu.make_async_copy(source, target, own_sem.at[2 * pair + half]))
            own[-1].start()
    for pair in range(2):
        for d in partners(me):
            for half in range(2):
                source = sorted_ref.at[rows_at(classes(d)[2 * pair + half] * 32, 32)]
                target = in1_ref.at[rows_at(pair * 2048 + me * 64 + half * 32, 32)]
                send(source, target, sems, pair, {"len": d})
    for pair in range(2):
        fill_levels(pair, me, roughness_ref, waviness_ref, coherence_ref, level_ref)
        fill_twist(pair, me, twist_ref)
    for load in loads:
        load.wait()
    for copy in own:
        copy.wait()

    own = []
    for pair in range(2):
        settle(in1_ref.at[pl.ds(0, 31 * 64)], sems, pair, other, 1)
        spectra(pair, in1_ref, level_ref, high_ref, low_ref)
        transforms(pair, me, high_ref, low_ref, row_ref, lane_ref, twist_ref, part_ref, out2_ref)
        span = pl.ds(64 * pair, 64)
        target = in2_ref.at[rows_at(me * 128 + 64 * pair, 64)]
        own.append(pltpu.make_async_copy(out2_ref.at[me, span], target, own_sem.at[4 + 2 * pair]))
        quarter = out2_ref.at[pl.ds(8 * plane, 8), span]
        target_mem = members_ref.at[plane, :, span]
        own.append(pltpu.make_async_copy(quarter, target_mem, own_sem.at[5 + 2 * pair]))
        own[-2].start()
        own[-1].start()
        for r in range(1, MEM):
            d = lax.rem(plane + r, MEM)
            send(out2_ref.at[pl.ds(8 * d, 8), span], target_mem, sems, 4 + pair, {"mem": d})
        for d in partners(me):
            send(out2_ref.at[d, span], target, sems, 2 + pair, {"len": d})
    for copy in own:
        copy.wait()

    for pair in range(2):
        settle(members_ref.at[pl.ds(0, 3), :, pl.ds(0, 64)], sems, 4 + pair, above, 1)
    mine_ref[...] = gram_part(members_ref, fold_ref, total_ref)
    grams_ref[me] = mine_ref[...]
    for d in partners(me):
        send(mine_ref, grams_ref.at[me], sems, 6, {"len": d})

    for pair in range(2):
        settle(in2_ref.at[pl.ds(0, 31 * 64)], sems, 2 + pair, other, 1)
    own = []
    for group in range(2):
        class_transform(group, in2_ref, class_ref, out3_ref)
        target = in3_ref.at[rows_at(group * 2048 + me * 64, 64)]
        own.append(
            pltpu.make_async_copy(out3_ref.at[rows_at(group * 2048 + me * 64, 64)], target, own_sem.at[8 + group])
        )
        own[-1].start()
        for d in partners(me):
            send(out3_ref.at[rows_at(group * 2048 + d * 64, 64)], target, sems, 7 + group, {"len": d})

    settle(grams_ref.at[pl.ds(0, 31)], sems, 6, other, 1)
    summed = lax.fori_loop(0, LEN, lambda n, total: total + grams_ref[n], jnp.zeros((8, LANES), F32))
    planes_ref[MEM] = summed
    planes_ref[plane] = summed
    for r in range(1, MEM):
        send(planes_ref.at[MEM], planes_ref.at[plane], sems, 9, {"mem": lax.rem(plane + r, MEM)})
    settle(planes_ref.at[pl.ds(0, 3)], sems, 9, above, 1)
    gram = planes_ref[0] + planes_ref[1] + planes_ref[2] + planes_ref[3]
    factor_ref[...] = upper_factor(gram)[:, :32]

    for copy in own:
        copy.wait()
    for group in range(2):
        settle(in3_ref.at[pl.ds(0, 31 * 64)], sems, 7 + group, other, 1)
        place(group, in3_ref, profile_ref)

    for pair in range(2):
        settle(in1_ref.at[pl.ds(0, 31 * 64)], sems, pair, other, 0)
        settle(in1_ref.at[pl.ds(0, 31 * 64)], sems, 2 + pair, other, 0)
        settle(members_ref.at[pl.ds(0, 3), :, pl.ds(0, 64)], sems, 4 + pair, above, 0)
        settle(in1_ref.at[pl.ds(0, 31 * 64)], sems, 7 + pair, other, 0)
    settle(grams_ref.at[pl.ds(0, 31)], sems, 6, other, 0)
    settle(planes_ref.at[pl.ds(0, 3)], sems, 9, above, 0)


def per_device(phase_left, phase_right, roughness, waviness, coherence):
    row_dft, lane_dft, class_dft, fold = tables()
    smem = pl.BlockSpec(memory_space=pltpu.SMEM)
    vmem = pl.BlockSpec(memory_space=pltpu.VMEM)
    hbm = pl.BlockSpec(memory_space=pl.ANY)
    return pl.pallas_call(
        road_kernel,
        out_shape=(jax.ShapeDtypeStruct((2, 8, 32768), F32), jax.ShapeDtypeStruct((32, 32), F32)),
        in_specs=[vmem, vmem, smem, smem, smem, hbm, hbm, hbm, hbm],
        out_specs=(vmem, vmem),
        scratch_shapes=[
            pltpu.VMEM(row_dft.shape, BF16),
            pltpu.VMEM(lane_dft.shape, BF16),
            pltpu.VMEM(class_dft.shape, BF16),
            pltpu.VMEM(fold.shape, F32),
            pltpu.VMEM((4096, LANES), F32),
            pltpu.VMEM((4096, LANES), F32),
            pltpu.VMEM((3, 2048, LANES), F32),
            pltpu.VMEM((2, 2048, LANES), F32),
            pltpu.VMEM((4, 2, 256, 256), BF16),
            pltpu.VMEM((4, 2, 256, 256), BF16),
            pltpu.VMEM((2, 2, 256, LANES), F32),
            pltpu.VMEM((LEN, 128, LANES), F32),
            pltpu.VMEM((4096, LANES), F32),
            pltpu.VMEM((MEM, 8, 128, LANES), F32),
            pltpu.VMEM((512, 512), F32),
            pltpu.VMEM((8, LANES), F32),
            pltpu.VMEM((LEN, 8, LANES), F32),
            pltpu.VMEM((MEM + 1, 8, LANES), F32),
            pltpu.VMEM((4096, LANES), F32),
            pltpu.VMEM((4096, LANES), F32),
            pltpu.SemaphoreType.DMA((4,)),
            pltpu.SemaphoreType.DMA((10,)),
            pltpu.SemaphoreType.DMA((2, 10)),
        ],
        compiler_params=pltpu.CompilerParams(
            collective_id=0, has_side_effects=True, vmem_limit_bytes=VMEM_LIMIT
        ),
        name="road_profiles",
    )(
        phase_left, phase_right, roughness, waviness, coherence,
        jnp.asarray(row_dft), jnp.asarray(lane_dft), jnp.asarray(class_dft), jnp.asarray(fold),
    )


def solution(mesh):
    placed = (P("mem", "len"), P("mem", "len"), P("mem"), P("mem"), P("mem"))
    return jax.shard_map(
        per_device,
        mesh=mesh,
        in_specs=placed,
        out_specs=(P(None, "mem", "len"), P()),
        check_vma=False,
    )
```

time: 596 us -> 97.5 us (0.16); the launches traced: 587 us -> 96.6 us
  matrix products: 190 us -> 0 us
  other arithmetic: 153 us -> 0 us
  local copies, waits for them, and re-layouts: 102 us -> 3.66 us
  Pallas kernels: 0 us -> 92.2 us
  blocking collectives: 58.7 us -> 0 us
  waiting for transfers between devices: 42.5 us -> 0 us
  starting transfers between devices: 26 us -> 0 us
  between operations: 14.5 us -> 0.65 us
    dot_general x69 -> x0, matrix products: 190 us -> none  [the longest x1 35.5 us: per_device(): first = jnp.einsum('jqa,qiac->cij', outer_cos, real_in, precision=highest)]
    another operation x96 -> x0, other arithmetic: 115 us -> none  [upper_of(): return jnp.linalg.cholesky(gram_matrix).T]
    pallas_call x0 -> x1, Pallas kernels: none -> 92.2 us  [per_device(): pl.pallas_call(road_kernel, out_shape=(jax.ShapeDtypeStruct((2, 8, 32768)...]
    reshape x8 -> x0, local copies, waits for them, and re-layouts: 46.2 us -> none  [the longest x2 18.2 us: per_device(): profile_block.reshape(columns, inner_block, shards, outer_block)]
    all_to_all x4 -> x0, waiting for transfers between devices: 42.5 us -> none  [the longest x1 28.1 us: per_device(): lax.all_to_all(outgoing, 'len', split_axis=0, concat_axis=0, tiled=True)]
    all_to_all x1 -> x0, blocking collectives: 35.5 us -> none  [per_device(): lax.all_to_all(rot_imag, 'len', split_axis=0, concat_axis=0, tiled=True)]
    all_to_all x4 -> x0, starting transfers between devices: 26 us -> none  [the longest x1 8.77 us: per_device(): lax.all_to_all(to_rows(real_part), 'len', split_axis=1, concat_axis=0, ti...]
    transpose x4 -> x0, local copies, waits for them, and re-layouts: 23.2 us -> none  [the longest x2 12.5 us: to_rows(): jnp.transpose(shaped, (2, 3, 0, 1))]
  transfers between devices with their start and end apart: 5 -> 0, of which waited for: 2 -> 0; matrix products, arithmetic and copies ran while one was open for 22% -> 0% of each run, Pallas kernels for 0% -> 0%
where the time goes in v2:
time: 97.5 us; the launch traced here: 96.6 us
  Pallas kernels  92.2 us (95%)
  local copies, waits for them, and re-layouts  3.66 us (4%)
    pallas_call x1, Pallas kernels, per_device(): pl.pallas_call(road_kernel, out_shape=(jax.ShapeDtypeStruct((2, 8, 32768)...  92.2 us
    unnamed x4, local copies, waits for them, and re-layouts  3.66 us

profile of v2, /device:TPU:1, one launch (start us, length us, event | category | flops | bytes accessed | tf_op | source)
XLA Modules:
  0.0 96.6 jit_solution(6133880496235447554)
XLA Ops:
  0.6 92.2 %road_profiles.1 = (f32[2,8,32768]{2,1,0:T(8,128)}, f32[32,32]{1,0:T(8,128)}) custom-call(f32[8,32768]{1,0:T(8,128)} %left_ref.1, f32[8,32768]{1,0:T(8,128)} %right_ref.1, f32[8]{0:T(128)} %roughness_ref.1, f32[8]{0:T(128)} %waviness_ref.1, f32[8]{0:T(128)} %coherence_ref.1, bf16[4,2,256,256]{3,2,1,0:T(8,128)(2,1)} %constant.8.clone.row_hbm, ...), custom_call_target="tpu_custom_call" | custom-call | tf_op jit(solution)/shard_map/road_profiles/pallas_call | solution.py:506
  92.9 0.0 copy-start
  92.9 3.1 %copy.13 = f32[2,8,32768]{2,1,0:T(8,128)} copy(f32[2,8,32768]{2,1,0:T(8,128)} %get-tuple-element.4) | data formatting | bytes 4194304
  95.9 0.0 copy-done
  95.9 0.6 copy.14
Async XLA Ops:
  92.9 3.1 %copy-start = (f32[32,32]{1,0:T(8,128)S(1)}, f32[32,32]{1,0:T(8,128)}, u32[]{:S(2)}) copy-start(f32[32,32]{1,0:T(8,128)} %get-tuple-element.5) | copy-start | bytes 12292

commit v3 on v2

--- a/solution.py
+++ b/solution.py
@@ -19,7 +19,7 @@
 F32 = jnp.float32
 BF16 = jnp.bfloat16
 MESH = pl.DeviceIdType.MESH
-VMEM_LIMIT = 56 * 1024 * 1024
+VMEM_LIMIT = 40 * 1024 * 1024
 
 
 def halves(table):
@@ -56,7 +56,7 @@
     cos, sin = 0.5 * same * np.cos(angle), 0.5 * same * np.sin(angle)
     lane_dft = halves(np.block([[cos, sin], [-sin, cos]]))
     v = np.arange(128)
-    c = class_of().reshape(-1)
+    c = class_of().reshape(LEN, 2, 2).transpose(2, 0, 1).reshape(-1)
     angle = turn * (v[:, None] * c[None, :] % 128) / 128.0
     cos, sin = np.cos(angle), np.sin(angle)
     class_dft = halves(np.block([[cos, -sin], [sin, cos]]))
@@ -148,7 +148,7 @@
         sorted_ref[pl.ds(index * 16 + i, 128, stride=32), :] = jnp.concatenate(tiles, axis=0).T
         return carry
 
-    lax.fori_loop(0, 16, step, 0)
+    lax.fori_loop(0, 16, step, 0, unroll=4)
 
 
 def member_lanes(ref):
@@ -289,9 +289,12 @@
             packed = [[jnp.where(is_first, alone[n][x], packed[n][x]) for x in range(2)] for n in range(2)]
         for n in range(2):
             for x in range(2):
-                start = (2 * pair + n) * 32 + x * 16
                 for wl in range(8):
-                    out_ref[4 * wl + a, start : start + 16, :] = packed[n][x][wl * 16 : wl * 16 + 16, :]
+                    for g in range(2):
+                        start = pair * 64 + g * 32 + n * 16 + x * 8
+                        out_ref[4 * wl + a, start : start + 8, :] = packed[n][x][
+                            wl * 16 + g * 8 : wl * 16 + g * 8 + 8, :
+                        ]
         return carry
 
     lax.fori_loop(0, 4, step, 0)
@@ -344,45 +347,41 @@
 
 
 def class_transform(group, in_ref, table_ref, out_ref):
-    def step(n, carry):
+    for n in range(2):
         columns = []
         for index in range(2):
-            u2 = group * 8 + 2 * n + index
-            re = in_ref[pl.ds(u2, 128, stride=32), :]
-            im = in_ref[pl.ds(16 + u2, 128, stride=32), :]
-            columns.append(jnp.concatenate([re, im], axis=0))
+            u2 = 4 * group + 2 * n + index
+            start = (u2 // 8) * 32 + u2 % 8
+            parts = [in_ref[pl.ds(start + 8 * x + 16 * half, 64, stride=64), :] for x in range(2) for half in range(2)]
+            columns.append(jnp.concatenate(parts, axis=0))
         high, low = split(jnp.concatenate(columns, axis=1))
         done = dot(table_ref[0], high) + dot(table_ref[1], high) + dot(table_ref[0], low)
         for index in range(2):
             for track in range(2):
-                out_ref[pl.ds(group * 2048 + 8 * track + 2 * n + index, 128, stride=16), :] = done[
+                out_ref[pl.ds(group * 1024 + 4 * track + 2 * n + index, 128, stride=8), :] = done[
                     track * 128 : track * 128 + 128, index * 128 : index * 128 + 128
                 ]
-        return carry
-
-    lax.fori_loop(0, 4, step, 0)
 
 
 def place(group, in_ref, out_ref):
     def step(index, carry):
-        vl = lax.div(index, 4)
-        track = lax.rem(lax.div(index, 2), 2)
-        high_u2 = lax.rem(index, 2)
-        base = group * 2048 + vl * 16 + track * 8 + high_u2 * 4
-        rows = [in_ref[pl.ds(base + low, 32, stride=64), :] for low in range(4)]
+        vl = lax.div(index, 2)
+        track = lax.rem(index, 2)
+        base = group * 1024 + vl * 8 + track * 4
+        rows = [in_ref[pl.ds(base + low, 32, stride=32), :] for low in range(4)]
         turned = jnp.concatenate(rows, axis=0).T
         for u3 in range(16):
-            column = pl.multiple_of((vl * 64 + u3 * 4 + group * 2 + high_u2) * 128, 128)
+            column = pl.multiple_of((vl * 64 + u3 * 4 + group) * 128, 128)
             out_ref[track, :, pl.ds(column, 128)] = turned[8 * u3 : 8 * u3 + 8, :]
         return carry
 
-    lax.fori_loop(0, 16, step, 0)
+    lax.fori_loop(0, 8, step, 0, unroll=2)
 
 
 def road_kernel(
-    left_ref, right_ref, roughness_ref, waviness_ref, coherence_ref, row_hbm, lane_hbm, class_hbm, fold_hbm,
+    left_hbm, right_hbm, roughness_ref, waviness_ref, coherence_ref, row_hbm, lane_hbm, class_hbm, fold_hbm,
     profile_ref, factor_ref,
-    row_ref, lane_ref, class_ref, fold_ref, sorted_ref, in1_ref, level_ref, twist_ref, high_ref, low_ref, part_ref,
+    left_ref, right_ref, row_ref, lane_ref, class_ref, fold_ref, sorted_ref, in1_ref, level_ref, twist_ref, high_ref, low_ref, part_ref,
     out2_ref, in2_ref, members_ref, total_ref, mine_ref, grams_ref, planes_ref, out3_ref, in3_ref,
     table_sem, own_sem, sems,
 ):
@@ -390,12 +389,9 @@
     plane = lax.axis_index("mem")
     other = {"len": lax.rem(me + 1, LEN)}
     above = {"mem": lax.rem(plane + 1, MEM)}
-    loads = [
-        pltpu.make_async_copy(source, target, table_sem.at[n])
-        for n, (source, target) in enumerate(
-            ((row_hbm, row_ref), (lane_hbm, lane_ref), (class_hbm, class_ref), (fold_hbm, fold_ref))
-        )
-    ]
+    pieces = [(left_hbm, left_ref), (right_hbm, right_ref)]
+    pieces += [(row_hbm, row_ref), (lane_hbm, lane_ref), (class_hbm, class_ref), (fold_hbm, fold_ref)]
+    loads = [pltpu.make_async_copy(source, target, table_sem.at[n]) for n, (source, target) in enumerate(pieces)]
     for load in loads:
         load.start()
     barrier = pltpu.get_barrier_semaphore()
@@ -407,7 +403,9 @@
     lax.fori_loop(1, LEN, greet, 0)
     for r in range(1, MEM):
         pl.semaphore_signal(barrier, inc=1, device_id={"mem": lax.rem(plane + r, MEM)}, device_id_type=MESH)
+    loads[0].wait()
     sort_phases(0, left_ref, sorted_ref)
+    loads[1].wait()
     sort_phases(1, right_ref, sorted_ref)
     pl.semaphore_wait(barrier, LEN + MEM - 2)
 
@@ -427,7 +425,7 @@
     for pair in range(2):
         fill_levels(pair, me, roughness_ref, waviness_ref, coherence_ref, level_ref)
         fill_twist(pair, me, twist_ref)
-    for load in loads:
+    for load in loads[2:]:
         load.wait()
     for copy in own:
         copy.wait()
@@ -448,8 +446,10 @@
         for r in range(1, MEM):
             d = lax.rem(plane + r, MEM)
             send(out2_ref.at[pl.ds(8 * d, 8), span], target_mem, sems, 4 + pair, {"mem": d})
-        for d in partners(me):
-            send(out2_ref.at[d, span], target, sems, 2 + pair, {"len": d})
+        for start, size, sem in ((0, 64, 2),) if pair == 0 else ((64, 32, 3), (96, 32, 10)):
+            for d in partners(me):
+                target = in2_ref.at[rows_at(me * 128 + start, size)]
+                send(out2_ref.at[d, pl.ds(start, size)], target, sems, sem, {"len": d})
     for copy in own:
         copy.wait()
 
@@ -460,18 +460,18 @@
     for d in partners(me):
         send(mine_ref, grams_ref.at[me], sems, 6, {"len": d})
 
-    for pair in range(2):
-        settle(in2_ref.at[pl.ds(0, 31 * 64)], sems, 2 + pair, other, 1)
+    settle(in2_ref.at[pl.ds(0, 31 * 64)], sems, 2, other, 1)
     own = []
-    for group in range(2):
+    for group in range(4):
+        if group % 2 == 0:
+            settle(in2_ref.at[pl.ds(0, 31 * 32)], sems, (3, 10)[group // 2], other, 1)
         class_transform(group, in2_ref, class_ref, out3_ref)
-        target = in3_ref.at[rows_at(group * 2048 + me * 64, 64)]
-        own.append(
-            pltpu.make_async_copy(out3_ref.at[rows_at(group * 2048 + me * 64, 64)], target, own_sem.at[8 + group])
-        )
+        target = in3_ref.at[rows_at(group * 1024 + me * 32, 32)]
+        mine = out3_ref.at[rows_at(group * 1024 + me * 32, 32)]
+        own.append(pltpu.make_async_copy(mine, target, own_sem.at[8 + group]))
         own[-1].start()
         for d in partners(me):
-            send(out3_ref.at[rows_at(group * 2048 + d * 64, 64)], target, sems, 7 + group, {"len": d})
+            send(out3_ref.at[rows_at(group * 1024 + d * 32, 32)], target, sems, 11 + group, {"len": d})
 
     settle(grams_ref.at[pl.ds(0, 31)], sems, 6, other, 1)
     summed = lax.fori_loop(0, LEN, lambda n, total: total + grams_ref[n], jnp.zeros((8, LANES), F32))
@@ -485,30 +485,62 @@
 
     for copy in own:
         copy.wait()
-    for group in range(2):
-        settle(in3_ref.at[pl.ds(0, 31 * 64)], sems, 7 + group, other, 1)
+    for group in range(4):
+        settle(in3_ref.at[pl.ds(0, 31 * 32)], sems, 11 + group, other, 1)
         place(group, in3_ref, profile_ref)
 
+    for sem, ref in ((0, in1_ref), (1, in1_ref), (2, in1_ref)):
+        settle(ref.at[pl.ds(0, 31 * 64)], sems, sem, other, 0)
+    for sem in (3, 10, 11, 12, 13, 14):
+        settle(in1_ref.at[pl.ds(0, 31 * 32)], sems, sem, other, 0)
     for pair in range(2):
-        settle(in1_ref.at[pl.ds(0, 31 * 64)], sems, pair, other, 0)
-        settle(in1_ref.at[pl.ds(0, 31 * 64)], sems, 2 + pair, other, 0)
         settle(members_ref.at[pl.ds(0, 3), :, pl.ds(0, 64)], sems, 4 + pair, above, 0)
-        settle(in1_ref.at[pl.ds(0, 31 * 64)], sems, 7 + pair, other, 0)
     settle(grams_ref.at[pl.ds(0, 31)], sems, 6, other, 0)
     settle(planes_ref.at[pl.ds(0, 3)], sems, 9, above, 0)
+
+
+def hand_over_kernel(profile_in, factor_in, profile_out, factor_out, sems):
+    copies = [
+        pltpu.make_async_copy(profile_in, profile_out, sems.at[0]),
+        pltpu.make_async_copy(factor_in, factor_out, sems.at[1]),
+    ]
+    for copy in copies:
+        copy.start()
+    for copy in copies:
+        copy.wait()
+
+
+def hand_over(profile, factor):
+    vmem = pl.BlockSpec(memory_space=pltpu.VMEM)
+    hbm = pl.BlockSpec(memory_space=pl.ANY)
+    return pl.pallas_call(
+        hand_over_kernel,
+        out_shape=(jax.ShapeDtypeStruct(profile.shape, F32), jax.ShapeDtypeStruct(factor.shape, F32)),
+        in_specs=[vmem, vmem],
+        out_specs=(hbm, hbm),
+        scratch_shapes=[pltpu.SemaphoreType.DMA((2,))],
+        compiler_params=pltpu.CompilerParams(vmem_limit_bytes=8 * 1024 * 1024),
+        name="hand_over",
+    )(profile, factor)
+
+
+def pinned(array):
+    return pltpu.with_memory_space_constraint(array, pltpu.HBM)
 
 
 def per_device(phase_left, phase_right, roughness, waviness, coherence):
     row_dft, lane_dft, class_dft, fold = tables()
     smem = pl.BlockSpec(memory_space=pltpu.SMEM)
     vmem = pl.BlockSpec(memory_space=pltpu.VMEM)
-    hbm = pl.BlockSpec(memory_space=pl.ANY)
-    return pl.pallas_call(
+    hbm = pl.BlockSpec(memory_space=pltpu.HBM)
+    profile, factor = pl.pallas_call(
         road_kernel,
         out_shape=(jax.ShapeDtypeStruct((2, 8, 32768), F32), jax.ShapeDtypeStruct((32, 32), F32)),
-        in_specs=[vmem, vmem, smem, smem, smem, hbm, hbm, hbm, hbm],
+        in_specs=[hbm, hbm, smem, smem, smem, hbm, hbm, hbm, hbm],
         out_specs=(vmem, vmem),
         scratch_shapes=[
+            pltpu.VMEM((8, 32768), F32),
+            pltpu.VMEM((8, 32768), F32),
             pltpu.VMEM(row_dft.shape, BF16),
             pltpu.VMEM(lane_dft.shape, BF16),
             pltpu.VMEM(class_dft.shape, BF16),
@@ -529,18 +561,19 @@
             pltpu.VMEM((MEM + 1, 8, LANES), F32),
             pltpu.VMEM((4096, LANES), F32),
             pltpu.VMEM((4096, LANES), F32),
-            pltpu.SemaphoreType.DMA((4,)),
-            pltpu.SemaphoreType.DMA((10,)),
-            pltpu.SemaphoreType.DMA((2, 10)),
+            pltpu.SemaphoreType.DMA((6,)),
+            pltpu.SemaphoreType.DMA((12,)),
+            pltpu.SemaphoreType.DMA((2, 15)),
         ],
         compiler_params=pltpu.CompilerParams(
             collective_id=0, has_side_effects=True, vmem_limit_bytes=VMEM_LIMIT
         ),
         name="road_profiles",
     )(
-        phase_left, phase_right, roughness, waviness, coherence,
-        jnp.asarray(row_dft), jnp.asarray(lane_dft), jnp.asarray(class_dft), jnp.asarray(fold),
+        *(pinned(array) for array in (phase_left, phase_right, roughness, waviness, coherence)),
+        *(pinned(jnp.asarray(table)) for table in (row_dft, lane_dft, class_dft, fold)),
     )
+    return hand_over(profile, factor)
 
 
 def solution(mesh):

time: 97.5 us -> 89.5 us (0.918)
  local copies, waits for them, and re-layouts: 3.66 us -> 0 us
  Pallas kernels: 92.2 us -> 88.8 us
    pallas_call x1, Pallas kernels: 92.2 us -> 87.4 us  [per_device(): pl.pallas_call(road_kernel, out_shape=(jax.ShapeDtypeStruct((2, 8, 32768)...]
    unnamed x4 -> x0, local copies, waits for them, and re-layouts: 3.66 us -> none
    pallas_call x0 -> x1, Pallas kernels: none -> 1.34 us  [hand_over(): pl.pallas_call(hand_over_kernel, out_shape=(jax.ShapeDtypeStruct(profile....]
where the time goes in v3:
time: 89.5 us; the launch traced here: 89.4 us
  Pallas kernels  88.8 us (99%)
    pallas_call x1, Pallas kernels, per_device(): pl.pallas_call(road_kernel, out_shape=(jax.ShapeDtypeStruct((2, 8, 32768)...  87.4 us

profile of v3, /device:TPU:1, one launch (start us, length us, event | category | flops | bytes accessed | tf_op | source)
XLA Modules:
  0.0 89.4 jit_solution(15998659905862614867)
XLA Ops:
  0.6 87.4 %road_profiles.1 = (f32[2,8,32768]{2,1,0:T(8,128)S(1)}, f32[32,32]{1,0:T(8,128)S(1)}) custom-call(f32[8,32768]{1,0:T(8,128)} %left_hbm.1, f32[8,32768]{1,0:T(8,128)} %right_hbm.1, f32[8]{0:T(128)} %roughness_ref.1, f32[8]{0:T(128)} %waviness_ref.1, f32[8]{0:T(128)} %coherence_ref.1, bf16[4,2,256,256]{3,2,1,0:T(8,128)(2,1)} %constant.8.clone.row_hbm, ...), custom_call_target="tpu_custom_call" | custom-call | tf_op jit(solution)/shard_map/road_profiles/pallas_call | solution.py:536
  88.1 1.3 %hand_over.1 = (f32[2,8,32768]{2,1,0:T(8,128)}, f32[32,32]{1,0:T(8,128)}) custom-call(f32[2,8,32768]{2,1,0:T(8,128)S(1)} %get-tuple-element.4.profile_in, f32[32,32]{1,0:T(8,128)S(1)} %get-tuple-element.5.factor_in), custom_call_target="tpu_custom_call" | custom-call | tf_op jit(solution)/shard_map/hand_over/pallas_call | solution.py:516

commit v4 on v3

--- a/solution.py
+++ b/solution.py
@@ -101,9 +101,9 @@
 
 
 def order():
-    ring = lambda n: min(n, 4 - n)
-    steps = [(dx, dy, dc) for dc in range(2) for dx in range(4) for dy in range(4) if (dx, dy, dc) != (0, 0, 0)]
-    return sorted(steps, key=lambda s: (-ring(s[0]) - ring(s[1]), s[2]))
+    chips = [(2, 2), (1, 2), (2, 1), (3, 2), (2, 3), (0, 2), (2, 0), (1, 1), (3, 3), (1, 3), (3, 1)]
+    chips += [(0, 1), (1, 0), (0, 3), (3, 0)]
+    return [(dx, dy, dc) for dc in range(2) for dx, dy in chips] + [(0, 0, 1)]
 
 
 def partners(me):
@@ -300,19 +300,23 @@
     lax.fori_loop(0, 4, step, 0)
 
 
-def gram_part(members_ref, fold_ref, total_ref):
-    total_ref[...] = jnp.zeros_like(total_ref)
+def gram_half(pair, members_ref, total_ref):
     product = functools.partial(
         lax.dot_general, dimension_numbers=(((0,), (0,)), ((), ())), preferred_element_type=F32
     )
 
-    def step(n, carry):
-        rows = [members_ref[z, pl.ds(2 * n, 2)].reshape(256, LANES) for z in range(MEM)]
+    def step(n):
+        span = pl.ds(64 * pair, 64)
+        rows = [members_ref[z, pl.ds(4 * n, 4), span].reshape(256, LANES) for z in range(MEM)]
         high, low = split(jnp.concatenate(rows, axis=1))
-        total_ref[...] += product(high, high) + product(low, high) + product(high, low)
-        return carry
-
-    lax.fori_loop(0, 4, step, 0)
+        part = product(high, high) + product(low, high) + product(high, low)
+        total_ref[...] = part if pair == 0 and n == 0 else total_ref[...] + part
+
+    step(0)
+    step(1)
+
+
+def gram_part(fold_ref, total_ref):
     row = lax.broadcasted_iota(jnp.int32, (512, 512), 0)
     column = lax.broadcasted_iota(jnp.int32, (512, 512), 1)
     same = lax.rem(lax.div(row, 8), 16) == lax.rem(lax.div(column, 8), 16)
@@ -336,11 +340,12 @@
 
     def step(n, carry):
         rest, upper = carry
+        column = jnp.sum(jnp.where(lane == n, rest, 0.0), axis=1, keepdims=True)
         line = jnp.sum(jnp.where(row == n, rest, 0.0), axis=0, keepdims=True)
-        column = jnp.sum(jnp.where(lane == n, rest, 0.0), axis=1, keepdims=True)
-        pivot = jnp.sum(jnp.where(lane[0:1] == n, line, 0.0), axis=1, keepdims=True)
-        line = jnp.where(lane[0:1] >= n, line / jnp.sqrt(pivot), 0.0)
-        column = column / jnp.sqrt(pivot)
+        pivot = jnp.sum(jnp.where(row[:, 0:1] == n, column, 0.0), axis=0, keepdims=True)
+        inverse = 1.0 / jnp.sqrt(pivot)
+        line = jnp.where(lane[0:1] >= n, line * inverse, 0.0)
+        column = column * inverse
         return rest - column * line, jnp.where(row == n, line, upper)
 
     return lax.fori_loop(0, 32, step, (matrix, jnp.zeros_like(matrix)))[1]
@@ -453,13 +458,8 @@
     for copy in own:
         copy.wait()
 
-    for pair in range(2):
-        settle(members_ref.at[pl.ds(0, 3), :, pl.ds(0, 64)], sems, 4 + pair, above, 1)
-    mine_ref[...] = gram_part(members_ref, fold_ref, total_ref)
-    grams_ref[me] = mine_ref[...]
-    for d in partners(me):
-        send(mine_ref, grams_ref.at[me], sems, 6, {"len": d})
-
+    settle(members_ref.at[pl.ds(0, 3), :, pl.ds(0, 64)], sems, 4, above, 1)
+    gram_half(0, members_ref, total_ref)
     settle(in2_ref.at[pl.ds(0, 31 * 64)], sems, 2, other, 1)
     own = []
     for group in range(4):
@@ -472,6 +472,13 @@
         own[-1].start()
         for d in partners(me):
             send(out3_ref.at[rows_at(group * 1024 + d * 32, 32)], target, sems, 11 + group, {"len": d})
+        if group == 1:
+            settle(members_ref.at[pl.ds(0, 3), :, pl.ds(0, 64)], sems, 5, above, 1)
+            gram_half(1, members_ref, total_ref)
+            mine_ref[...] = gram_part(fold_ref, total_ref)
+            grams_ref[me] = mine_ref[...]
+            for d in partners(me):
+                send(mine_ref, grams_ref.at[me], sems, 6, {"len": d})
 
     settle(grams_ref.at[pl.ds(0, 31)], sems, 6, other, 1)
     summed = lax.fori_loop(0, LEN, lambda n, total: total + grams_ref[n], jnp.zeros((8, LANES), F32))
@@ -479,15 +486,15 @@
     planes_ref[plane] = summed
     for r in range(1, MEM):
         send(planes_ref.at[MEM], planes_ref.at[plane], sems, 9, {"mem": lax.rem(plane + r, MEM)})
-    settle(planes_ref.at[pl.ds(0, 3)], sems, 9, above, 1)
-    gram = planes_ref[0] + planes_ref[1] + planes_ref[2] + planes_ref[3]
-    factor_ref[...] = upper_factor(gram)[:, :32]
-
     for copy in own:
         copy.wait()
     for group in range(4):
         settle(in3_ref.at[pl.ds(0, 31 * 32)], sems, 11 + group, other, 1)
         place(group, in3_ref, profile_ref)
+        if group == 0:
+            settle(planes_ref.at[pl.ds(0, 3)], sems, 9, above, 1)
+            gram = planes_ref[0] + planes_ref[1] + planes_ref[2] + planes_ref[3]
+            factor_ref[...] = upper_factor(gram)[:, :32]
 
     for sem, ref in ((0, in1_ref), (1, in1_ref), (2, in1_ref)):
         settle(ref.at[pl.ds(0, 31 * 64)], sems, sem, other, 0)

time: 89.5 us -> 83.3 us (0.931)
  Pallas kernels: 88.8 us -> 82.5 us
    pallas_call x1, Pallas kernels: 87.4 us -> 81.2 us  [per_device(): pl.pallas_call(road_kernel, out_shape=(jax.ShapeDtypeStruct((2, 8, 32768)...]
where the time goes in v4:
time: 83.3 us; the launch traced here: 83.1 us
  Pallas kernels  82.5 us (99%)
    pallas_call x1, Pallas kernels, per_device(): pl.pallas_call(road_kernel, out_shape=(jax.ShapeDtypeStruct((2, 8, 32768)...  81.2 us

profile of v4, /device:TPU:1, one launch (start us, length us, event | category | flops | bytes accessed | tf_op | source)
XLA Modules:
  0.0 83.1 jit_solution(16530628507035233969)
XLA Ops:
  0.6 81.2 %road_profiles.1 = (f32[2,8,32768]{2,1,0:T(8,128)S(1)}, f32[32,32]{1,0:T(8,128)S(1)}) custom-call(f32[8,32768]{1,0:T(8,128)} %left_hbm.1, f32[8,32768]{1,0:T(8,128)} %right_hbm.1, f32[8]{0:T(128)} %roughness_ref.1, f32[8]{0:T(128)} %waviness_ref.1, f32[8]{0:T(128)} %coherence_ref.1, bf16[4,2,256,256]{3,2,1,0:T(8,128)(2,1)} %constant.8.clone.row_hbm, ...), custom_call_target="tpu_custom_call" | custom-call | tf_op jit(solution)/shard_map/road_profiles/pallas_call | solution.py:543
  81.8 1.3 %hand_over.1 = (f32[2,8,32768]{2,1,0:T(8,128)}, f32[32,32]{1,0:T(8,128)}) custom-call(f32[2,8,32768]{2,1,0:T(8,128)S(1)} %get-tuple-element.4.profile_in, f32[32,32]{1,0:T(8,128)S(1)} %get-tuple-element.5.factor_in), custom_call_target="tpu_custom_call" | custom-call | tf_op jit(solution)/shard_map/hand_over/pallas_call | solution.py:523

commit v5 on v4

--- a/solution.py
+++ b/solution.py
@@ -19,6 +19,7 @@
 F32 = jnp.float32
 BF16 = jnp.bfloat16
 MESH = pl.DeviceIdType.MESH
+PIECES = 4
 VMEM_LIMIT = 40 * 1024 * 1024
 
 
@@ -142,13 +143,12 @@
     return -cos, -sin
 
 
-def sort_phases(index, ref, sorted_ref):
-    def step(i, carry):
-        tiles = [ref[:, pl.ds(pl.multiple_of(i * 2048 + e * 128, 128), 128)] for e in range(16)]
-        sorted_ref[pl.ds(index * 16 + i, 128, stride=32), :] = jnp.concatenate(tiles, axis=0).T
-        return carry
-
-    lax.fori_loop(0, 16, step, 0, unroll=4)
+def sort_phases(index, load, ref, sorted_ref):
+    for piece in range(PIECES):
+        load[piece].wait()
+        for i in range(piece * 16 // PIECES, (piece + 1) * 16 // PIECES):
+            tiles = [ref[:, i * 2048 + e * 128 : i * 2048 + e * 128 + 128] for e in range(16)]
+            sorted_ref[pl.ds(index * 16 + i, 128, stride=32), :] = jnp.concatenate(tiles, axis=0).T
 
 
 def member_lanes(ref):
@@ -394,7 +394,11 @@
     plane = lax.axis_index("mem")
     other = {"len": lax.rem(me + 1, LEN)}
     above = {"mem": lax.rem(plane + 1, MEM)}
-    pieces = [(left_hbm, left_ref), (right_hbm, right_ref)]
+    pieces = []
+    for source, target in ((left_hbm, left_ref), (right_hbm, right_ref)):
+        for n in range(PIECES):
+            span = pl.ds(n * (32768 // PIECES), 32768 // PIECES)
+            pieces.append((source.at[:, span], target.at[:, span]))
     pieces += [(row_hbm, row_ref), (lane_hbm, lane_ref), (class_hbm, class_ref), (fold_hbm, fold_ref)]
     loads = [pltpu.make_async_copy(source, target, table_sem.at[n]) for n, (source, target) in enumerate(pieces)]
     for load in loads:
@@ -408,10 +412,8 @@
     lax.fori_loop(1, LEN, greet, 0)
     for r in range(1, MEM):
         pl.semaphore_signal(barrier, inc=1, device_id={"mem": lax.rem(plane + r, MEM)}, device_id_type=MESH)
-    loads[0].wait()
-    sort_phases(0, left_ref, sorted_ref)
-    loads[1].wait()
-    sort_phases(1, right_ref, sorted_ref)
+    sort_phases(0, loads[:PIECES], left_ref, sorted_ref)
+    sort_phases(1, loads[PIECES:], right_ref, sorted_ref)
     pl.semaphore_wait(barrier, LEN + MEM - 2)
 
     own = []
@@ -430,7 +432,7 @@
     for pair in range(2):
         fill_levels(pair, me, roughness_ref, waviness_ref, coherence_ref, level_ref)
         fill_twist(pair, me, twist_ref)
-    for load in loads[2:]:
+    for load in loads[2 * PIECES :]:
         load.wait()
     for copy in own:
         copy.wait()
@@ -568,7 +570,7 @@
             pltpu.VMEM((MEM + 1, 8, LANES), F32),
             pltpu.VMEM((4096, LANES), F32),
             pltpu.VMEM((4096, LANES), F32),
-            pltpu.SemaphoreType.DMA((6,)),
+            pltpu.SemaphoreType.DMA((2 * PIECES + 4,)),
             pltpu.SemaphoreType.DMA((12,)),
             pltpu.SemaphoreType.DMA((2, 15)),
         ],

time: 83.3 us -> 83.3 us (level)
  no operation moved by 1% of the time
where the time goes in v5:
time: 83.3 us; the launch traced here: 83.2 us
  Pallas kernels  82.5 us (99%)
    pallas_call x1, Pallas kernels, per_device(): pl.pallas_call(road_kernel, out_shape=(jax.ShapeDtypeStruct((2, 8, 32768)...  81.2 us

profile of v5, /device:TPU:1, one launch (start us, length us, event | category | flops | bytes accessed | tf_op | source)
XLA Modules:
  0.0 83.2 jit_solution(12295398584208866467)
XLA Ops:
  0.6 81.2 %road_profiles.1 = (f32[2,8,32768]{2,1,0:T(8,128)S(1)}, f32[32,32]{1,0:T(8,128)S(1)}) custom-call(f32[8,32768]{1,0:T(8,128)} %left_hbm.1, f32[8,32768]{1,0:T(8,128)} %right_hbm.1, f32[8]{0:T(128)} %roughness_ref.1, f32[8]{0:T(128)} %waviness_ref.1, f32[8]{0:T(128)} %coherence_ref.1, bf16[4,2,256,256]{3,2,1,0:T(8,128)(2,1)} %constant.8.clone.row_hbm, ...), custom_call_target="tpu_custom_call" | custom-call | tf_op jit(solution)/shard_map/road_profiles/pallas_call | solution.py:545
  81.8 1.3 %hand_over.1 = (f32[2,8,32768]{2,1,0:T(8,128)}, f32[32,32]{1,0:T(8,128)}) custom-call(f32[2,8,32768]{2,1,0:T(8,128)S(1)} %get-tuple-element.4.profile_in, f32[32,32]{1,0:T(8,128)S(1)} %get-tuple-element.5.factor_in), custom_call_target="tpu_custom_call" | custom-call | tf_op jit(solution)/shard_map/hand_over/pallas_call | solution.py:525
